TPU v7x, 128 devices: a whole 4x4x4 slice. The times are simulated.
128 devices in a mesh: fsdp: 4 (over z_hi, core), seq: 32 (over y, x, z_lo).
Axes of the slice: x: 4, y: 4, z: 4 (z_hi: 2, z_lo: 2; z = z_hi * 2 + z_lo), core: 2. Of those that a mesh axis runs over, the one named last changes fastest.
Arguments:
- tokens: bfloat16 [4, 8192, 5376], P('fsdp', 'seq'), may hold values from -6 to 6
- norm_gain: float32 [5376], replicated, may hold values from 0.25 to 1.75
- w_query: bfloat16 [5376, 2048], P('fsdp', 'seq'), may hold values from -0.078125 to 0.078125
- w_keyval: bfloat16 [5376, 2048], P('fsdp', 'seq'), may hold values from -0.078125 to 0.078125
- q_gain: float32 [128], replicated, may hold values from 0.5 to 9
- k_gain: float32 [128], replicated, may hold values from 0.5 to 9
Outputs:
- attended: bfloat16 [4, 8192, 2048], P('fsdp', 'seq')
All inputs are finite; a program needn't handle non-finite values.
Results may differ from a plain program's by a relative error of at most 0.004.
The roundings to bfloat16 on the way count: a program that leaves them out, or rounds other values in their place, can miss the bound.
Values may be sent and summed in bfloat16 or wider, within the bound.
A program may use at most 128 MiB of HBM per device.

v0:
```python
import jax
import jax.numpy as jnp
from jax import lax
from jax.sharding import PartitionSpec as P

WINDOW = 1024
QSCALE = 168


def from_behind(value, axis, by):
    size = lax.axis_size(axis)
    pairs = [(i, i + by) for i in range(size) if 0 <= i + by < size]
    return lax.ppermute(value, axis, pairs)


def head_norm(values, gain):
    return values * lax.rsqrt(jnp.mean(values * values, axis=-1, keepdims=True) + 1e-06) * gain


def rotate(values, position):
    half = values.shape[-1] // 2
    index_f = jnp.arange(half).astype(jnp.float32)
    freq = jnp.power(10000.0, -2.0 * index_f / values.shape[-1])
    angle = position[:, None] * freq[None, :]
    cosine = jnp.cos(angle)[:, None, :]
    sine = jnp.sin(angle)[:, None, :]
    first = values[..., :half]
    second = values[..., half:]
    return jnp.concatenate(
        [first * cosine - second * sine, second * cosine + first * sine], axis=-1
    )


def column_terms(spread, piece):
    return jnp.dot(spread, piece, preferred_element_type=jnp.float32)


def query_terms(spread, w_query):
    return column_terms(spread, lax.all_gather(w_query, "seq", axis=1, tiled=True))


def keyval_terms(spread, w_keyval):
    return column_terms(spread, lax.all_gather(w_keyval, "seq", axis=1, tiled=True))


def fetch_window(local, reach):
    pieces = []
    for hop in range(reach, 0, -1):
        pieces.append(from_behind(local, "seq", hop))
    return jnp.concatenate(pieces + [local], axis=0)


def on_device(tokens, norm_gain, w_query, w_keyval, q_gain, k_gain):
    rows = tokens.shape[1]
    head_dim = q_gain.shape[0]
    seq_count = lax.axis_size("seq")
    q_width = w_query.shape[1] * seq_count
    kv_width = w_keyval.shape[1] * seq_count // 2
    heads_q = q_width // head_dim
    heads_kv = kv_width // head_dim
    groups = heads_q // heads_kv
    reach = WINDOW // rows
    scale = float(QSCALE) ** (-0.5)
    flat = tokens[0].astype(jnp.float32)
    normed = (
        flat * lax.rsqrt(jnp.mean(flat * flat, axis=-1, keepdims=True) + 1e-06) * norm_gain
    ).astype(jnp.bfloat16)
    spread = lax.all_to_all(normed, "fsdp", split_axis=1, concat_axis=0, tiled=True)
    owner = lax.axis_index("seq")
    query_pos = owner * rows + jnp.arange(rows)
    position = query_pos.astype(jnp.float32)
    q_part = query_terms(spread, w_query)
    kv_part = keyval_terms(spread, w_keyval)
    query_sum, keyval_sum = (
        lax.psum_scatter(q_part, "fsdp", scatter_dimension=0, tiled=True),
        lax.psum_scatter(kv_part, "fsdp", scatter_dimension=0, tiled=True),
    )
    keys = rotate(
        head_norm(keyval_sum[:, :kv_width].reshape(rows, heads_kv, head_dim), k_gain), position
    )
    values = lax.optimization_barrier(keyval_sum[:, kv_width:].astype(jnp.bfloat16)).astype(
        jnp.float32
    )
    keyval = jnp.concatenate([keys.reshape(rows, kv_width), values], axis=1)
    query = rotate(head_norm(query_sum.reshape(rows, heads_q, head_dim), q_gain), position)
    window = fetch_window(keyval, reach)
    span = window.shape[0]
    key_pos = (owner - reach) * rows + jnp.arange(span)
    gap = query_pos[:, None] - key_pos[None, :]
    allowed = (gap >= 0) & (gap < WINDOW) & (key_pos[None, :] >= 0)
    keys_all = window[:, :kv_width].reshape(span, heads_kv, head_dim)
    values_all = window[:, kv_width:].astype(jnp.bfloat16).reshape(span, heads_kv, head_dim)
    grouped = query.reshape(rows, heads_kv, groups, head_dim)

    def one_head(head):
        q_head = lax.dynamic_index_in_dim(grouped, head, 1, keepdims=False)
        k_head = lax.dynamic_index_in_dim(keys_all, head, 1, keepdims=False)
        v_head = lax.dynamic_index_in_dim(values_all, head, 1, keepdims=False)
        scores = jnp.einsum("tgd,kd->gtk", q_head, k_head, precision=lax.Precision.HIGHEST) * scale
        masked = jnp.where(allowed[None], scores, -1e30)
        top = jnp.max(masked, axis=-1, keepdims=True)
        weights = jnp.where(allowed[None], jnp.exp(masked - top), 0.0)
        probs = (weights / jnp.sum(weights, axis=-1, keepdims=True)).astype(jnp.bfloat16)
        result = jnp.einsum("gtk,kd->tgd", probs, v_head, preferred_element_type=jnp.float32)
        return result.astype(jnp.bfloat16)

    heads_out = lax.map(one_head, jnp.arange(heads_kv))
    return heads_out.transpose(1, 0, 2, 3).reshape(1, rows, heads_q * head_dim)


def solution(mesh):
    in_specs = (P("fsdp", "seq", None), P(), P("fsdp", "seq"), P("fsdp", "seq"), P(), P())
    out_specs = P("fsdp", "seq", None)
    return jax.shard_map(
        on_device, mesh=mesh, in_specs=in_specs, out_specs=out_specs, check_vma=False
    )
```

profile of v0, /device:TPU:8, one launch (start us, length us, event | category | flops | bytes accessed | tf_op | source)
XLA Modules:
  0.0 746.2 jit_solution(6908857002582597282)
XLA Ops:
  8.1 3.3 copy.29
  13.1 97.4 %all_to_all.16 = bf16[256,4,1344]{0,2,1:T(8,128)(2,1)S(1)} all-to-all(bf16[256,4,1344]{0,2,1:T(8,128)(2,1)S(1)} %multiply_convert_fusion), channel_id=1, replica_groups=mesh['fsdp'=4,'seq'=32] {'fsdp'}, dimensions={1} | all-to-all | bytes 5505024 | tf_op jit(solution)/shard_map/all_to_all | solution.py:68
  110.6 2.8 copy.30
  113.4 67.4 %all-gather.3.cloned.1.call-done = bf16[1344,2048]{0,1:T(8,128)(2,1)} async-done(((bf16[1344,64]{0,1:T(8,128)(2,1)}), bf16[1344,2048]{0,1:T(8,128)(2,1)}) %all-gather.3.cloned.1.call-update) | async-done | bytes 5505040 | tf_op jit(solution)/shard_map/all_gather | solution.py:43
  180.8 11.6 %fusion.22 = f32[1024,2048]{1,0:T(8,128)} fusion(bf16[1024,1344]{1,0:T(8,128)(2,1)} %bitcast.77, bf16[1344,2048]{0,1:T(8,128)(2,1)} %all-gather.3.cloned.1.call-done), kind=kOutput, calls=%fused_computation.58 | convolution fusion | flops 5637144576 | bytes 16646144 | tf_op jit(solution)/shard_map/dot_general | solution.py:35
  192.5 150.9 %all-gather.5.cloned.1.call-done = bf16[1344,2048]{0,1:T(8,128)(2,1)} async-done(((bf16[1344,64]{0,1:T(8,128)(2,1)}), bf16[1344,2048]{0,1:T(8,128)(2,1)}) %all-gather.5.cloned.1.call-update) | async-done | bytes 5505040 | tf_op jit(solution)/shard_map/all_gather | solution.py:39
  343.4 10.8 %fusion.23 = f32[1024,2048]{1,0:T(8,128)} fusion(bf16[1024,1344]{1,0:T(8,128)(2,1)S(1)} %bitcast.78, bf16[1344,2048]{0,1:T(8,128)(2,1)} %all-gather.5.cloned.1.call-done), kind=kOutput, calls=%fused_computation.59 | convolution fusion | flops 5637144576 | bytes 16646144 | tf_op jit(solution)/shard_map/dot_general | solution.py:35
  354.9 76.3 %reduce-scatter.3.cloned.1.call-done = f32[256,2048]{1,0:T(8,128)} async-done(((f32[1024,2048]{1,0:T(8,128)}), f32[256,2048]{1,0:T(8,128)}) %reduce-scatter.3.cloned.1.call-update) | async-done | bytes 2097168 | tf_op jit(solution)/shard_map/reduce_scatter | solution.py:76
  438.6 4.9 collective-permute-start
  446.1 3.0 collective-permute-start.2
  449.1 4.8 collective-permute-start.3
  453.9 136.2 %reduce-scatter.5.cloned.1.call-done = f32[256,2048]{1,0:T(8,128)} async-done(((f32[1024,2048]{1,0:T(8,128)}), f32[256,2048]{1,0:T(8,128)}) %reduce-scatter.5.cloned.1.call-update) | async-done | bytes 2097168 | tf_op jit(solution)/shard_map/reduce_scatter | solution.py:75
  605.7 19.6 %collective-permute-done.3 = f32[256,2048]{1,0:T(8,128)} collective-permute-done((f32[256,2048]{1,0:T(8,128)}, f32[256,2048]{1,0:T(8,128)}, u32[]{:S(2)}, u32[]{:S(2)}) %collective-permute-start.3) | collective-permute-done | bytes 2097184 | tf_op jit(solution)/shard_map/ppermute | solution.py:13
  628.6 3.6 copy.45
  634.9 102.5 %while.11 = (s32[]{:T(128)}, bf16[8,256,2,128]{1,3,2,0:T(8,128)(2,1)}, s32[8]{0:T(128)S(1)}, bf16[1280,8,128]{0,2,1:T(8,128)(2,1)}, f32[1280,8,128]{2,1,0:T(8,12...) while((s32[]{:T(128)}, ...), condition=%wide.region_8.9_spmd.clone, body=%wide.region_5.8_spmd.clone.sunk | while | flops 1180697856 | bytes 14167983 | solution.py:107
  641.2 3.3 fusion.43
  650.3 2.8 constant_dynamic-slice_fusion.2
  654.1 3.3 fusion.43
  666.9 3.3 fusion.43
  679.7 3.3 fusion.43
  692.5 3.3 fusion.43
  705.3 3.3 fusion.43
  718.1 3.3 fusion.43
  730.9 3.3 fusion.43
  (103 shorter events, 94.8 us)
Async XLA Ops:
  6.5 174.3 %all-gather.3.cloned.1.call-start = ((), (), s32[]{:S(2)}) async-start(), calls=%async_computation.3 | async-start | bytes 5947392 | tf_op jit(solution)/shard_map/all_gather | solution.py:43
  7.3 336.2 %all-gather.5.cloned.1.call-start = ((), (), s32[]{:S(2)}) async-start(), calls=%async_computation.5 | async-start | bytes 5947392 | tf_op jit(solution)/shard_map/all_gather | solution.py:39
  8.0 3.4 copy-start.3
  8.0 423.2 %reduce-scatter.3.cloned.1.call-start = ((), (), s32[]{:S(2)}) async-start(), calls=%async_computation.4 | async-start | bytes 10485760 | tf_op jit(solution)/shard_map/reduce_scatter | solution.py:76
  192.4 151.0 %copy-start.2 = (bf16[4,256,1344]{2,1,0:T(8,128)(2,1)S(1)}, bf16[4,256,1344]{2,1,0:T(8,128)(2,1)}, u32[]{:S(2)}) copy-start(bf16[4,256,1344]{2,1,0:T(8,128)(2,1)} %copy.30) | copy-start | bytes 8257540
  192.5 397.6 %reduce-scatter.5.cloned.1.call-start = ((), (), s32[]{:S(2)}) async-start(), calls=%async_computation.6 | async-start | bytes 10485760 | tf_op jit(solution)/shard_map/reduce_scatter | solution.py:75
  354.8 78.4 %copy-start.4 = (f32[128]{0:T(128)S(1)}, f32[128]{0:T(128)}, u32[]{:S(2)}) copy-start(f32[128]{0:T(128)} %param.13) | copy-start | bytes 1540
  436.2 1.0 copy-start
  438.6 161.7 %collective-permute-start = (f32[256,2048]{1,0:T(8,128)}, f32[256,2048]{1,0:T(8,128)}, u32[]{:S(2)}, u32[]{:S(2)}) collective-permute-start(f32[256,2048]{1,0:T(8,128)} %pad_maximum_fusion), channel_id=1, source_target_pairs={{0,4},{1,5},{2,6},{3,7},{4,8},{5,9},{6,10},{7,11},{8,12},{9,13},{1... | collective-permute-start | bytes 6291464 | tf_op jit(solution)/shard_map/ppermute | solution.py:13
  443.5 158.6 %collective-permute-start.1 = (f32[256,2048]{1,0:T(8,128)}, f32[256,2048]{1,0:T(8,128)}, u32[]{:S(2)}, u32[]{:S(2)}) collective-permute-start(f32[256,2048]{1,0:T(8,128)} %pad_maximum_fusion), channel_id=1, source_target_pairs={{0,3},{1,4},{2,5},{3,6},{4,7},{5,8},{6,9},{7,10},{8,11},{9,12},{10... | collective-permute-start | bytes 6291464 | tf_op jit(solution)/shard_map/ppermute | solution.py:13
  446.1 157.9 %collective-permute-start.2 = (f32[256,2048]{1,0:T(8,128)}, f32[256,2048]{1,0:T(8,128)}, u32[]{:S(2)}, u32[]{:S(2)}) collective-permute-start(f32[256,2048]{1,0:T(8,128)} %pad_maximum_fusion), channel_id=1, source_target_pairs={{0,2},{1,3},{2,4},{3,5},{4,6},{5,7},{6,8},{7,9},{8,10},{9,11},{10,... | collective-permute-start | bytes 6291464 | tf_op jit(solution)/shard_map/ppermute | solution.py:13
  449.1 176.3 %collective-permute-start.3 = (f32[256,2048]{1,0:T(8,128)}, f32[256,2048]{1,0:T(8,128)}, u32[]{:S(2)}, u32[]{:S(2)}) collective-permute-start(f32[256,2048]{1,0:T(8,128)} %pad_maximum_fusion), channel_id=1, source_target_pairs={{0,1},{1,2},{2,3},{3,4},{4,5},{5,6},{6,7},{7,8},{8,9},{9,10},{10,1... | collective-permute-start | bytes 6291464 | tf_op jit(solution)/shard_map/ppermute | solution.py:13
  605.7 21.4 %copy-start.1 = (f32[256,1024]{1,0:T(8,128)S(1)}, f32[256,1024]{1,0:T(8,128)}, u32[]{:S(2)}) copy-start(f32[256,1024]{1,0:T(8,128)} %copy-done) | copy-start | bytes 3145732
Sparse Core Ops, SparseCore 0:
  9.0 171.7 all-gather.2
  182.4 160.9 all-gather.4
  346.1 85.0 reduce-scatter.2
  433.7 156.3 reduce-scatter.4
where the time goes:
time: 748 us; the launch traced here: 746 us
  waiting for transfers between devices  452 us (60%)
  blocking collectives  97.4 us (13%)
  matrix products  65.3 us (9%)
  local copies, waits for them, and re-layouts  59.8 us (8%)
  other arithmetic  27.2 us (4%)
  loops' own time  15.8 us (2%)
  starting transfers between devices  15.3 us (2%)
  between operations  13.5 us (2%)
    all_gather x1, waiting for transfers between devices, query_terms(): lax.all_gather(w_query, 'seq', axis=1, tiled=True)  151 us
    reduce_scatter x1, waiting for transfers between devices, on_device(): lax.psum_scatter(q_part, 'fsdp', scatter_dimension=0, tiled=True)  136 us
    all_to_all x1, blocking collectives, on_device(): lax.all_to_all(normed, 'fsdp', split_axis=1, concat_axis=0, tiled=True)  97.4 us
    reduce_scatter x1, waiting for transfers between devices, on_device(): lax.psum_scatter(kv_part, 'fsdp', scatter_dimension=0, tiled=True)  76.3 us
    all_gather x1, waiting for transfers between devices, keyval_terms(): lax.all_gather(w_keyval, 'seq', axis=1, tiled=True)  67.4 us
    dot_general x8, matrix products, one_head(): jnp.einsum('tgd,kd->gtk', q_head, k_head, precision=lax.Precision.HIGHEST)  26.7 us
    dot_general x2, matrix products, column_terms(): return jnp.dot(spread, piece, preferred_element_type=jnp.float32)  22.5 us
    dynamic_slice x8, local copies, waits for them, and re-layouts, one_head(): k_head = lax.dynamic_index_in_dim(keys_all, head, 1, keepdims=False)  22.3 us
  transfers between devices with their start and end apart: 8, of which 5 were waited for; matrix products, arithmetic and copies ran while one was open for 7% of the time, Pallas kernels for 0%

commit v1 on v0

v1 whole, which is shorter than its diff:
```python
import functools
import math

import jax
import jax.numpy as jnp
from jax import lax
from jax.experimental import pallas as pl
from jax.experimental.pallas import tpu as pltpu
from jax.sharding import PartitionSpec as P

WINDOW = 1024
QSCALE = 168
MESH = pl.DeviceIdType.MESH
F32 = jnp.float32
BF16 = jnp.bfloat16
NEG = -1e30

ORDERS = (("x", "y", "z"), ("y", "z", "x"), ("z", "x", "y"))


def position():
    f, s = lax.axis_index("fsdp"), lax.axis_index("seq")
    return {"x": (s // 2) % 4, "y": s // 8, "z": 2 * (f // 2) + s % 2}, f % 2


def device(at, core):
    return (2 * (at["z"] // 2) + core, 8 * at["y"] + 2 * at["x"] + at["z"] % 2)


def shifted(at, dim, by):
    moved = dict(at)
    moved[dim] = (at[dim] + by + 4) % 4
    return moved


def project_kernel(
    tok_ref, gain_ref, shard_ref, cos_ref, sin_ref, ga_ref, gb_ref,
    q_ref, kv_ref,
    w0, w1, w2, normed, spread, acc, other, local_sem, ring_send, ring_recv,
    tok_send, tok_recv, part_send, part_recv,
):
    at, core = position()
    me = device(at, core)
    partner = device(at, 1 - core)
    rows = tok_ref.shape[0]
    third = w0.shape[3]
    weights = (w0, w1, w2)

    barrier = pltpu.get_barrier_semaphore()
    peers = [device(shifted(at, d, by), core) for d in "xyz" for by in (1, -1)] + [partner]
    for peer in peers:
        pl.semaphore_signal(barrier, inc=1, device_id=peer, device_id_type=MESH)

    own = []
    for c, (d1, d2, d3) in enumerate(ORDERS):
        own.append(pltpu.make_async_copy(
            shard_ref.at[c], weights[c].at[at[d3], at[d2], at[d1]], local_sem.at[c]))
        own[-1].start()
    for copy in own:
        copy.wait()
    pl.semaphore_wait(barrier, len(peers))

    sent = []

    def view(c, phase, index, half):
        d1, d2, d3 = ORDERS[c]
        w = weights[c]
        if phase == 0:
            if half is None:
                return w.at[at[d3], at[d2], index]
            return w.at[at[d3], at[d2], index, pl.ds(half * (third // 2), third // 2)]
        if phase == 1:
            if half is None:
                return w.at[at[d3], index]
            return w.at[at[d3], index, pl.ds(2 * half, 2)]
        if half is None:
            return w.at[index]
        return w.at[index, pl.ds(2 * half, 2)]

    def ring(c, phase, step):
        dim = ORDERS[c][phase]
        copies = []
        for side, by in enumerate((1, -1)):
            if step == 0:
                block = view(c, phase, at[dim], None)
            else:
                block = view(c, phase, shifted(at, dim, -by)[dim], side)
            copies.append(pltpu.make_async_remote_copy(
                src_ref=block, dst_ref=block,
                send_sem=ring_send.at[c, phase, step, side],
                recv_sem=ring_recv.at[c, phase, step, side],
                device_id=device(shifted(at, dim, by), core), device_id_type=MESH))
        return copies

    def start(copies):
        for copy in copies:
            copy.start()
        sent.extend(copies)

    flying = [ring(c, 0, 0) for c in range(3)]
    for copies in flying:
        start(copies)
    for phase in range(3):
        for step in range(2):
            if (phase, step) == (2, 0):
                break
            later = (phase, 1) if step == 0 else (phase + 1, 0)
            for c in range(3):
                for copy in flying[c]:
                    copy.wait_recv()
                flying[c] = ring(c, *later)
                start(flying[c])

    strip = 32

    def norm_rows(i, _):
        at_row = pl.ds(pl.multiple_of(i * strip, strip), strip)
        flat = tok_ref[at_row, :].astype(F32)
        mean = jnp.mean(flat * flat, axis=-1, keepdims=True)
        out = (flat * lax.rsqrt(mean + 1e-6) * gain_ref[...]).astype(BF16)
        for q in range(4):
            for c in range(3):
                k = q * 3 + c
                normed[q, c, at_row, :] = out[:, k * third:(k + 1) * third]
        return 0

    lax.fori_loop(0, rows // strip, norm_rows, 0)
    exchange = []
    for zh in range(2):
        pltpu_copy = pltpu.make_async_copy(
            normed.at[2 * zh + core], spread.at[zh, core], local_sem.at[3 + zh])
        pltpu_copy.start()
        remote = pltpu.make_async_remote_copy(
            src_ref=normed.at[2 * zh + 1 - core], dst_ref=spread.at[zh, core],
            send_sem=tok_send.at[zh], recv_sem=tok_recv.at[zh],
            device_id=partner, device_id_type=MESH)
        remote.start()
        exchange.append((pltpu_copy, remote))
    for mine, remote in exchange:
        mine.wait()
        remote.wait()

    x, y, zown = at["x"], at["y"], at["z"] // 2

    def weight(c, z, yy, xx):
        index = {"x": xx, "y": yy, "z": z}
        d1, d2, d3 = ORDERS[c]
        return weights[c][index[d3], index[d2], index[d1]]

    def units(yy, xx, parts, first):
        h = 4 * yy + xx
        for slab in range(2):
            total = None
            for c, zh in parts:
                rhs = jnp.concatenate(
                    [weight(c, 2 * zh, yy, xx), weight(c, 2 * zh + 1, yy, xx)], axis=1)
                term = jnp.dot(spread[zh, slab, c], rhs, preferred_element_type=F32)
                total = term if total is None else total + term
            if first:
                acc[h, slab] = total
            else:
                acc[h, slab] += total

    def near(k):
        return k + k // 2

    zfar = 1 - zown
    both = lambda c: [(c, 0), (c, 1)]

    def wait_ring():
        for c in range(3):
            for copy in flying[c]:
                copy.wait_recv()

    wait_ring()
    for c in range(3):
        flying[c] = ring(c, 2, 1)
        start(flying[c])

    def early_near(i, _):
        units((y + near(i // 3)) % 4, (x + near(i % 3)) % 4, [(0, zown)] + both(1) + both(2), True)
        return 0

    def early_x(i, _):
        units((y + near(i)) % 4, (x + 2) % 4, [(0, zown)] + both(2), True)
        return 0

    def early_y(i, _):
        units((y + 2) % 4, (x + near(i)) % 4, [(0, zown)] + both(1), True)
        return 0

    lax.fori_loop(0, 9, early_near, 0)
    lax.fori_loop(0, 3, early_x, 0)
    lax.fori_loop(0, 3, early_y, 0)
    units((y + 2) % 4, (x + 2) % 4, [(0, zown)], True)
    wait_ring()

    def part(h):
        return pltpu.make_async_remote_copy(
            src_ref=acc.at[h, 1 - core], dst_ref=other.at[h],
            send_sem=part_send.at[h], recv_sem=part_recv.at[h],
            device_id=partner, device_id_type=MESH)

    def late(h):
        part(h).start()

    def late_near(i, _):
        yy, xx = (y + near(i // 3)) % 4, (x + near(i % 3)) % 4
        units(yy, xx, [(0, zfar)], False)
        late(4 * yy + xx)
        return 0

    def late_x(i, _):
        yy, xx = (y + near(i)) % 4, (x + 2) % 4
        units(yy, xx, [(0, zfar)] + both(1), False)
        late(4 * yy + xx)
        return 0

    def late_y(i, _):
        yy, xx = (y + 2) % 4, (x + near(i)) % 4
        units(yy, xx, [(0, zfar)] + both(2), False)
        late(4 * yy + xx)
        return 0

    lax.fori_loop(0, 9, late_near, 0)
    lax.fori_loop(0, 3, late_x, 0)
    lax.fori_loop(0, 3, late_y, 0)
    units((y + 2) % 4, (x + 2) % 4, [(0, zfar)] + both(1) + both(2), False)
    late(4 * ((y + 2) % 4) + (x + 2) % 4)

    half = 64
    low = lax.broadcasted_iota(jnp.int32, (rows, 2 * half), 1) < half

    def head(h, is_key):
        part(h).wait_recv()
        p0 = acc[h, core, :, 0:128] + other[h, :, 0:128]
        p1 = acc[h, core, :, 128:256] + other[h, :, 128:256]
        squares = p0 * p0 + p1 * p1
        mean_q = jnp.sum(jnp.where(low, squares, 0.0), axis=-1, keepdims=True) / 128.0
        rq = lax.rsqrt(mean_q + 1e-6)
        if is_key:
            mean_k = jnp.sum(jnp.where(low, 0.0, squares), axis=-1, keepdims=True) / 128.0
            r = jnp.where(low, rq, lax.rsqrt(mean_k + 1e-6))
        else:
            r = rq
        n0 = p0 * r * ga_ref[...]
        n1 = p1 * r * gb_ref[...]
        cos, sin = cos_ref[...], sin_ref[...]
        r0 = n0 * cos - n1 * sin
        r1 = n1 * cos + n0 * sin
        q = jnp.where(low, r0, pltpu.roll(r1, half, 1)) * (QSCALE ** -0.5 * math.log2(math.e))
        q_hi = q.astype(BF16)
        q_ref[h, :, 0:128] = q_hi
        q_ref[h, :, 128:256] = (q - q_hi.astype(F32)).astype(BF16)
        if is_key:
            k = jnp.where(low, pltpu.roll(r0, half, 1), r1)
            k_hi = k.astype(BF16)
            kv_ref[h, :, 0:128] = k_hi
            kv_ref[h, :, 128:256] = (k - k_hi.astype(F32)).astype(BF16)
        else:
            v = jnp.where(low, pltpu.roll(p0, half, 1), p1)
            kv_ref[h - 8, :, 256:384] = v.astype(BF16)

    def key_head(h, _):
        head(h, True)
        return 0

    def value_head(h, _):
        head(h, False)
        return 0

    lax.fori_loop(0, 8, key_head, 0)
    lax.fori_loop(8, 16, value_head, 0)
    for copy in sent:
        copy.wait_send()

    def drain(h, _):
        part(h).wait_send()
        return 0

    lax.fori_loop(0, 16, drain, 0)


def attend_kernel(q_ref, own_ref, out_ref, kv, own_sem, send_sem, recv_sem):
    f, s = lax.axis_index("fsdp"), lax.axis_index("seq")
    zlo = s % 2
    count = lax.axis_size("seq")
    rows = own_ref.shape[1]
    groups = 4
    per = own_ref.shape[0] // groups
    ahead, pair = s + 2, s + 1 - 2 * zlo

    barrier = pltpu.get_barrier_semaphore()

    def greet(target):
        pl.semaphore_signal(barrier, inc=1, device_id=(f, target), device_id_type=MESH)

    for target in (pair, (s + 2) % count, (s - 2 + count) % count):
        greet(target)

    own = pltpu.make_async_copy(own_ref, kv.at[0], own_sem)
    own.start()

    def clear(slot, absent):
        @pl.when(absent)
        def _():
            kv[slot] = jnp.zeros(kv.shape[1:], BF16)

    clear(1, s < 1)
    clear(2, s < 2)
    clear(3, s < 3)
    clear(4, s < 4)
    own.wait()
    pl.semaphore_wait(barrier, 3)

    def move(src, dst, group, target):
        block = pl.ds(group * per, per)
        return pltpu.make_async_remote_copy(
            src_ref=kv.at[src, block], dst_ref=kv.at[dst, block],
            send_sem=send_sem.at[dst, group], recv_sem=recv_sem.at[dst, group],
            device_id=(f, target), device_id_type=MESH)

    def arrived(slot, group):
        move(slot, slot, group, pair).wait_recv()

    sends = (
        (ahead < count, 0, 2, ahead),
        ((s >= 2) & (ahead < count), 2, 4, ahead),
        (zlo == 0, 0, 1, pair),
        ((zlo == 0) & (s >= 2), 2, 3, pair),
        ((zlo == 1) & (s >= 2), 2, 1, pair),
        ((zlo == 1) & (s >= 4), 4, 3, pair),
    )

    def send(which, group):
        condition, src, dst, target = sends[which]

        @pl.when(condition)
        def _():
            move(src, dst, group, target).start()

    def drain(which, group):
        condition, src, dst, target = sends[which]

        @pl.when(condition)
        def _():
            move(src, dst, group, target).wait_send()

    def receive(slot, group):
        @pl.when(s >= slot)
        def _():
            arrived(slot, group)

    row = lax.broadcasted_iota(jnp.int32, (rows, rows), 0)
    col = lax.broadcasted_iota(jnp.int32, (rows, rows), 1)
    causal = col <= row
    contract = (((1,), (1,)), ((), ()))
    pen = [jnp.where(s >= slot, 0.0, NEG).astype(F32) for slot in range(5)]

    def query_head(h, k):
        q_hi, q_lo = q_ref[h, :, 0:128], q_ref[h, :, 128:256]
        q_hi, q_lo = jnp.concatenate([q_hi, q_hi], 1), jnp.concatenate([q_lo, q_lo], 1)

        def score(slot):
            keys = kv[slot, k, :, 0:256]
            return (lax.dot_general(q_hi, keys, contract, preferred_element_type=F32)
                    + lax.dot_general(q_lo, keys, contract, preferred_element_type=F32))

        edge = jnp.where(causal, score(0), score(4) + pen[4])
        inner = [score(slot) for slot in (1, 2, 3)]
        top = jnp.max(edge, axis=-1, keepdims=True)
        for slot in (1, 2, 3):
            top = jnp.maximum(top, jnp.max(inner[slot - 1], axis=-1, keepdims=True) + pen[slot])
        w_edge = jnp.exp2(edge - top)
        w_inner = [jnp.exp2(inner[slot - 1] - (top - pen[slot])) for slot in (1, 2, 3)]
        total = jnp.sum(w_edge, axis=-1, keepdims=True)
        for w in w_inner:
            total = total + jnp.sum(w, axis=-1, keepdims=True)
        inv = 1.0 / total
        p_edge = w_edge * inv
        out = jnp.dot(jnp.where(causal, p_edge, 0.0).astype(BF16), kv[0, k, :, 256:384],
                      preferred_element_type=F32)
        out += jnp.dot(jnp.where(causal, 0.0, p_edge).astype(BF16), kv[4, k, :, 256:384],
                       preferred_element_type=F32)
        for slot in (1, 2, 3):
            out += jnp.dot((w_inner[slot - 1] * inv).astype(BF16), kv[slot, k, :, 256:384],
                           preferred_element_type=F32)
        out_ref[:, pl.ds(pl.multiple_of(h * 128, 128), 128)] = out.astype(BF16)

    def attend(group):
        def body(i, _):
            h = group * per * 2 + i
            query_head(h, h // 2)
            return 0

        lax.fori_loop(0, 2 * per, body, 0)

    for g in (0, 1):
        send(0, g)
        send(2, g)
    for g in range(groups):
        receive(2, g)
        send(1, g)
        send(3, g)
        send(4, g)
        if g + 2 < groups:
            send(0, g + 2)
            send(2, g + 2)
        receive(4, g)
        send(5, g)
        if g >= 1:
            receive(1, g - 1)
            receive(3, g - 1)
            attend(g - 1)
    receive(1, groups - 1)
    receive(3, groups - 1)
    attend(groups - 1)
    for which in range(len(sends)):
        for g in range(groups):
            drain(which, g)


def on_device(tokens, norm_gain, w_query, w_keyval, q_gain, k_gain):
    rows, width = tokens.shape[1:]
    quarter, cols = w_query.shape
    heads = cols * lax.axis_size("seq") // q_gain.shape[0]
    half = q_gain.shape[0] // 2
    third = quarter // 3
    shard = jnp.concatenate([w_query, w_keyval], axis=1).reshape(3, third, 2 * cols)
    place = (lax.axis_index("seq") * rows + jnp.arange(rows)).astype(F32)
    freq = jnp.power(10000.0, -2.0 * jnp.arange(half).astype(F32) / (2 * half))
    angle = place[:, None] * freq[None, :]
    cos = jnp.tile(jnp.cos(angle), (1, 2))
    sin = jnp.tile(jnp.sin(angle), (1, 2))
    ga = jnp.concatenate([q_gain[:half], k_gain[:half]])[None]
    gb = jnp.concatenate([q_gain[half:], k_gain[half:]])[None]
    vmem = pl.BlockSpec(memory_space=pltpu.VMEM)
    anyspace = pl.BlockSpec(memory_space=pl.ANY)
    dma = pltpu.SemaphoreType.DMA
    block = pltpu.VMEM((4, 4, 4, third, 128), BF16)
    q, kv = pl.pallas_call(
        project_kernel,
        name="project",
        out_shape=(
            jax.ShapeDtypeStruct((heads, rows, 256), BF16),
            jax.ShapeDtypeStruct((heads // 2, rows, 384), BF16),
        ),
        in_specs=[vmem, vmem, anyspace, vmem, vmem, vmem, vmem],
        out_specs=(vmem, vmem),
        scratch_shapes=[
            block, block, block,
            pltpu.VMEM((4, 3, rows, third), BF16),
            pltpu.VMEM((2, 2, 3, rows, third), BF16),
            pltpu.VMEM((heads, 2, rows, 256), F32),
            pltpu.VMEM((heads, rows, 256), F32),
            dma((5,)), dma((3, 3, 2, 2)), dma((3, 3, 2, 2)),
            dma((2,)), dma((2,)), dma((heads,)), dma((heads,)),
        ],
        compiler_params=pltpu.CompilerParams(
            collective_id=0, has_side_effects=True, vmem_limit_bytes=63 * 2**20),
    )(tokens[0], norm_gain[None], shard, cos, sin, ga, gb)
    out = pl.pallas_call(
        attend_kernel,
        name="attend",
        out_shape=jax.ShapeDtypeStruct((rows, heads * 128), BF16),
        in_specs=[vmem, anyspace],
        out_specs=vmem,
        scratch_shapes=[
            pltpu.VMEM((5, heads // 2, rows, 384), BF16),
            dma, dma((5, 4)), dma((5, 4)),
        ],
        compiler_params=pltpu.CompilerParams(
            collective_id=1, has_side_effects=True, vmem_limit_bytes=48 * 2**20),
    )(q, kv)
    return out[None]


def solution(mesh):
    in_specs = (P("fsdp", "seq", None), P(), P("fsdp", "seq"), P("fsdp", "seq"), P(), P())
    out_specs = P("fsdp", "seq", None)
    return jax.shard_map(
        on_device, mesh=mesh, in_specs=in_specs, out_specs=out_specs, check_vma=False
    )
```

time: 748 us -> 212 us (0.28)
  waiting for transfers between devices: 452 us -> 0 us
  Pallas kernels: 0 us -> 198 us
  blocking collectives: 97.4 us -> 0 us
  matrix products: 65.3 us -> 0 us
  local copies, waits for them, and re-layouts: 59.8 us -> 9.35 us
  other arithmetic: 27.2 us -> 1.97 us
  loops' own time: 15.8 us -> 0 us
  starting transfers between devices: 15.3 us -> 0 us
  between operations: 13.5 us -> 0.05 us
    all_gather x2 -> x0, waiting for transfers between devices: 218 us -> none  [the longest x1 151 us: query_terms(): lax.all_gather(w_query, 'seq', axis=1, tiled=True)]
    reduce_scatter x2 -> x0, waiting for transfers between devices: 213 us -> none  [the longest x1 136 us: on_device(): lax.psum_scatter(q_part, 'fsdp', scatter_dimension=0, tiled=True)]
    pallas_call x0 -> x2, Pallas kernels: none -> 198 us  [the longest x1 105 us: on_device(): pl.pallas_call(project_kernel, name='project', out_shape=(jax.ShapeDtypeS...]
    all_to_all x1 -> x0, blocking collectives: 97.4 us -> none  [on_device(): lax.all_to_all(normed, 'fsdp', split_axis=1, concat_axis=0, tiled=True)]
    dot_general x18 -> x0, matrix products: 65.3 us -> none  [the longest x8 26.7 us: one_head(): jnp.einsum('tgd,kd->gtk', q_head, k_head, precision=lax.Precision.HIGHEST)]
    dynamic_slice x16 -> x0, local copies, waits for them, and re-layouts: 27 us -> none  [the longest x8 22.3 us: one_head(): k_head = lax.dynamic_index_in_dim(keys_all, head, 1, keepdims=False)]
    ppermute x4 -> x0, waiting for transfers between devices: 19.6 us -> none  [from_behind(): return lax.ppermute(value, axis, pairs)]
    unnamed x22 -> x5, local copies, waits for them, and re-layouts: 22.3 us -> 3.96 us
  transfers between devices with their start and end apart: 8 -> 0, of which waited for: 5 -> 0; matrix products, arithmetic and copies ran while one was open for 7% -> 0% of each run, Pallas kernels for 0% -> 0%
where the time goes in v1:
time: 212 us; the launch traced here: 209 us
  Pallas kernels  198 us (93%)
  local copies, waits for them, and re-layouts  9.35 us (4%)
    pallas_call x1, Pallas kernels, on_device(): pl.pallas_call(project_kernel, name='project', out_shape=(jax.ShapeDtypeS...  105 us
    pallas_call x1, Pallas kernels, on_device(): pl.pallas_call(attend_kernel, name='attend', out_shape=jax.ShapeDtypeStru...  92.4 us

profile of v1, /device:TPU:8, one launch (start us, length us, event | category | flops | bytes accessed | tf_op | source)
XLA Modules:
  0.0 209.0 jit_solution(4869794767742742624)
XLA Ops:
  0.0 0.8 fusion
  0.8 0.8 fusion.1
  1.6 0.6 maximum_bitcast_fusion
  2.2 1.4 broadcast_in_dim.14.gain_ref
  3.6 0.3 multiply_sine_fusion
  3.9 0.7 copy.10.sin_ref
  4.7 0.7 copy.9.cos_ref
  5.4 1.0 pad_maximum_fusion
  6.5 0.9 copy.8
  7.4 105.2 %project.1 = (bf16[16,256,256]{2,1,0:T(8,128)(2,1)}, bf16[8,256,384]{2,1,0:T(8,128)(2,1)}) custom-call(bf16[256,5376]{1,0:T(8,128)(2,1)} %bitcast.10, f32[1,5376]{1,0:T(1,128)} %broadcast_in_dim.14.gain_ref, bf16[3,448,128]{2,1,0:T(8,128)(2,1)} %bitcast.11, f32[256,128]{1,0:T(8,128)} %copy.9.cos_ref, f32[256,128]{1,0:T(8,128)} %copy.10.sin_ref, ...), custom_call_target="tpu_custom_call" | custom-call | tf_op jit(solution)/shard_map/project/pallas_call | solution.py:441
  112.6 0.0 copy-start
  112.6 1.6 copy-done
  114.2 0.0 copy-start.1
  114.2 1.4 copy-done.1
  115.6 92.4 %attend.1 = bf16[256,2048]{1,0:T(8,128)(2,1)S(1)} custom-call(bf16[16,256,256]{2,1,0:T(8,128)(2,1)S(1)} %copy-done, bf16[8,256,384]{2,1,0:T(8,128)(2,1)S(1)} %copy-done.1), custom_call_target="tpu_custom_call" | custom-call | tf_op jit(solution)/shard_map/attend/pallas_call | solution.py:462
  208.0 1.0 copy.12
  (4 shorter events, 0.0 us)
Async XLA Ops:
  112.6 1.6 copy-start
  114.2 1.4 copy-start.1

commit v2 on v1

--- a/solution.py
+++ b/solution.py
@@ -33,11 +33,12 @@
     return moved
 
 
-def project_kernel(
+def layer_kernel(
     tok_ref, gain_ref, shard_ref, cos_ref, sin_ref, ga_ref, gb_ref,
-    q_ref, kv_ref,
-    w0, w1, w2, normed, spread, acc, other, local_sem, ring_send, ring_recv,
-    tok_send, tok_recv, part_send, part_recv,
+    out_ref,
+    w0, w1, w2, normed, spread, acc, other, q_own, q_in, kv_out, kv, relay, result,
+    local_sem, ring_send, ring_recv, tok_send, tok_recv, part_send, part_recv,
+    pair_send, pair_recv, x_send, x_recv, relay_recv, out_send, out_recv,
 ):
     at, core = position()
     me = device(at, core)
@@ -45,11 +46,33 @@
     rows = tok_ref.shape[0]
     third = w0.shape[3]
     weights = (w0, w1, w2)
+    f, s = lax.axis_index("fsdp"), lax.axis_index("seq")
+    zlo = s % 2
+    run = s // 2
+    runs = 16
+
+    relayed = 4 * at["y"] + (at["x"] + 1) % 4
+    relay_to = (f, 2 * ((relayed + 2) % runs) + zlo)
+    relay_by = device(shifted(at, "x", -1), core)
+    ahead = (f, (s + 2) % (2 * runs))
+    behind = (f, (s - 2 + 2 * runs) % (2 * runs))
+    pair = (f, s + 1 - 2 * zlo)
+    source = (run - 2 + runs) % runs
+    relay_from = (f, 2 * (4 * (source // 4) + (source + 3) % 4) + zlo)
 
     barrier = pltpu.get_barrier_semaphore()
-    peers = [device(shifted(at, d, by), core) for d in "xyz" for by in (1, -1)] + [partner]
+    peers = [device(shifted(at, d, by), core) for d in "xyz" for by in (1, -1)]
+    peers += [partner, ahead, behind, relay_to, relay_from]
     for peer in peers:
         pl.semaphore_signal(barrier, inc=1, device_id=peer, device_id_type=MESH)
+
+    def clear(first, absent):
+        @pl.when(absent)
+        def _():
+            kv[:, first:first + 2] = jnp.zeros((4, 2) + kv.shape[2:], BF16)
+
+    clear(0, run < 2)
+    clear(2, run < 1)
 
     own = []
     for c, (d1, d2, d3) in enumerate(ORDERS):
@@ -231,7 +254,7 @@
     half = 64
     low = lax.broadcasted_iota(jnp.int32, (rows, 2 * half), 1) < half
 
-    def head(h, is_key):
+    def head(h, keep_kv, is_key):
         part(h).wait_recv()
         p0 = acc[h, core, :, 0:128] + other[h, :, 0:128]
         p1 = acc[h, core, :, 128:256] + other[h, :, 128:256]
@@ -250,174 +273,181 @@
         r1 = n1 * cos + n0 * sin
         q = jnp.where(low, r0, pltpu.roll(r1, half, 1)) * (QSCALE ** -0.5 * math.log2(math.e))
         q_hi = q.astype(BF16)
-        q_ref[h, :, 0:128] = q_hi
-        q_ref[h, :, 128:256] = (q - q_hi.astype(F32)).astype(BF16)
+        q_own[h, :, 0:128] = q_hi
+        q_own[h, :, 128:256] = (q - q_hi.astype(F32)).astype(BF16)
         if is_key:
             k = jnp.where(low, pltpu.roll(r0, half, 1), r1)
             k_hi = k.astype(BF16)
-            kv_ref[h, :, 0:128] = k_hi
-            kv_ref[h, :, 128:256] = (k - k_hi.astype(F32)).astype(BF16)
+            keep_kv[:, 0:128] = k_hi
+            keep_kv[:, 128:256] = (k - k_hi.astype(F32)).astype(BF16)
         else:
             v = jnp.where(low, pltpu.roll(p0, half, 1), p1)
-            kv_ref[h - 8, :, 256:384] = v.astype(BF16)
-
-    def key_head(h, _):
-        head(h, True)
-        return 0
-
-    def value_head(h, _):
-        head(h, False)
-        return 0
-
-    lax.fori_loop(0, 8, key_head, 0)
-    lax.fori_loop(8, 16, value_head, 0)
-    for copy in sent:
-        copy.wait_send()
-
-    def drain(h, _):
-        part(h).wait_send()
-        return 0
-
-    lax.fori_loop(0, 16, drain, 0)
-
-
-def attend_kernel(q_ref, own_ref, out_ref, kv, own_sem, send_sem, recv_sem):
-    f, s = lax.axis_index("fsdp"), lax.axis_index("seq")
-    zlo = s % 2
-    count = lax.axis_size("seq")
-    rows = own_ref.shape[1]
-    groups = 4
-    per = own_ref.shape[0] // groups
-    ahead, pair = s + 2, s + 1 - 2 * zlo
-
-    barrier = pltpu.get_barrier_semaphore()
-
-    def greet(target):
-        pl.semaphore_signal(barrier, inc=1, device_id=(f, target), device_id_type=MESH)
-
-    for target in (pair, (s + 2) % count, (s - 2 + count) % count):
-        greet(target)
-
-    own = pltpu.make_async_copy(own_ref, kv.at[0], own_sem)
-    own.start()
-
-    def clear(slot, absent):
-        @pl.when(absent)
-        def _():
-            kv[slot] = jnp.zeros(kv.shape[1:], BF16)
-
-    clear(1, s < 1)
-    clear(2, s < 2)
-    clear(3, s < 3)
-    clear(4, s < 4)
-    own.wait()
-    pl.semaphore_wait(barrier, 3)
-
-    def move(src, dst, group, target):
-        block = pl.ds(group * per, per)
+            keep_kv[:, 256:384] = v.astype(BF16)
+
+    def remote(src, dst, send_sem, recv_sem, to):
         return pltpu.make_async_remote_copy(
-            src_ref=kv.at[src, block], dst_ref=kv.at[dst, block],
-            send_sem=send_sem.at[dst, group], recv_sem=recv_sem.at[dst, group],
-            device_id=(f, target), device_id_type=MESH)
-
-    def arrived(slot, group):
-        move(slot, slot, group, pair).wait_recv()
-
-    sends = (
-        (ahead < count, 0, 2, ahead),
-        ((s >= 2) & (ahead < count), 2, 4, ahead),
-        (zlo == 0, 0, 1, pair),
-        ((zlo == 0) & (s >= 2), 2, 3, pair),
-        ((zlo == 1) & (s >= 2), 2, 1, pair),
-        ((zlo == 1) & (s >= 4), 4, 3, pair),
-    )
-
-    def send(which, group):
-        condition, src, dst, target = sends[which]
-
+            src_ref=src, dst_ref=dst, send_sem=send_sem, recv_sem=recv_sem,
+            device_id=to, device_id_type=MESH)
+
+    def over_pair(g):
+        return remote(kv_out.at[g], kv.at[g, 4 + zlo], pair_send.at[0, g], pair_recv.at[0, g], pair)
+
+    def query_pair(g):
+        mine = pl.ds(8 * (1 - zlo) + 2 * g, 2)
+        return remote(q_own.at[mine], q_in.at[pl.ds(2 * g, 2)],
+                      pair_send.at[1, g], pair_recv.at[1, g], pair)
+
+    def next_run(g, block):
+        return remote(kv.at[g, 4 + block], kv.at[g, 2 + block],
+                      x_send.at[block, g], x_recv.at[2 + block, g], ahead)
+
+    def second_run(g):
+        return remote(kv.at[g, 2], kv.at[g, 0], x_send.at[2, g], x_recv.at[0, g], ahead)
+
+    def to_relay(g):
+        return remote(kv.at[g, 5], relay.at[g], x_send.at[3, g], relay_recv.at[g], relay_by)
+
+    def from_relay(g):
+        return remote(relay.at[g], kv.at[g, 1], x_send.at[4, g], x_recv.at[1, g], relay_to)
+
+    def when(condition, action):
         @pl.when(condition)
         def _():
-            move(src, dst, group, target).start()
-
-    def drain(which, group):
-        condition, src, dst, target = sends[which]
-
-        @pl.when(condition)
-        def _():
-            move(src, dst, group, target).wait_send()
-
-    def receive(slot, group):
-        @pl.when(s >= slot)
-        def _():
-            arrived(slot, group)
+            action()
+
+    has_next, has_second = run + 1 < runs, run + 2 < runs
+    relays = relayed + 2 < runs
+
+    def send_own(g):
+        when(has_next, next_run(g, zlo).start)
+        when(has_second & (zlo == 1), to_relay(g).start)
+
+    def hop(g):
+        over_pair(g).wait_recv()
+        when(has_next, next_run(g, 1 - zlo).start)
+        when(has_second & (zlo == 0), to_relay(g).start)
+
+    def forward(g):
+        when(run >= 1, next_run(g, 0).wait_recv)
+        when((run >= 1) & has_next, second_run(g).start)
+        when(relays, to_relay(g).wait_recv)
+        when(relays, from_relay(g).start)
+
+    def epilogue(g, _):
+        for mine in (True, False):
+            k = 4 * zlo + g if mine else 4 * (1 - zlo) + g
+            keep = kv.at[g, 4 + zlo] if mine else kv_out.at[g]
+            head(k, keep, True)
+            head(8 + k, keep, False)
+        over_pair(g).start()
+        when(g < 2, lambda: send_own(g))
+        return 0
+
+    lax.fori_loop(0, 4, epilogue, 0)
+    for g in range(4):
+        query_pair(g).start()
 
     row = lax.broadcasted_iota(jnp.int32, (rows, rows), 0)
     col = lax.broadcasted_iota(jnp.int32, (rows, rows), 1)
     causal = col <= row
     contract = (((1,), (1,)), ((), ()))
-    pen = [jnp.where(s >= slot, 0.0, NEG).astype(F32) for slot in range(5)]
-
-    def query_head(h, k):
-        q_hi, q_lo = q_ref[h, :, 0:128], q_ref[h, :, 128:256]
+
+    def query_head(g, token_block, q, keep):
+        q_hi, q_lo = q[:, 0:128], q[:, 128:256]
         q_hi, q_lo = jnp.concatenate([q_hi, q_hi], 1), jnp.concatenate([q_lo, q_lo], 1)
-
-        def score(slot):
-            keys = kv[slot, k, :, 0:256]
+        pen = [jnp.where(2 * run - 4 + token_block + m >= 0, 0.0, NEG).astype(F32)
+               for m in range(5)]
+
+        def score(m):
+            keys = kv[g, token_block + m, :, 0:256]
             return (lax.dot_general(q_hi, keys, contract, preferred_element_type=F32)
                     + lax.dot_general(q_lo, keys, contract, preferred_element_type=F32))
 
-        edge = jnp.where(causal, score(0), score(4) + pen[4])
-        inner = [score(slot) for slot in (1, 2, 3)]
+        def attend_to(probs, m):
+            return jnp.dot(probs.astype(BF16), kv[g, token_block + m, :, 256:384],
+                           preferred_element_type=F32)
+
+        edge = jnp.where(causal, score(4), score(0) + pen[0])
+        inner = {m: score(m) for m in (1, 2, 3)}
         top = jnp.max(edge, axis=-1, keepdims=True)
-        for slot in (1, 2, 3):
-            top = jnp.maximum(top, jnp.max(inner[slot - 1], axis=-1, keepdims=True) + pen[slot])
+        for m in inner:
+            top = jnp.maximum(top, jnp.max(inner[m], axis=-1, keepdims=True) + pen[m])
         w_edge = jnp.exp2(edge - top)
-        w_inner = [jnp.exp2(inner[slot - 1] - (top - pen[slot])) for slot in (1, 2, 3)]
+        w_inner = {m: jnp.exp2(inner[m] - (top - pen[m])) for m in inner}
         total = jnp.sum(w_edge, axis=-1, keepdims=True)
-        for w in w_inner:
-            total = total + jnp.sum(w, axis=-1, keepdims=True)
+        for m in inner:
+            total = total + jnp.sum(w_inner[m], axis=-1, keepdims=True)
         inv = 1.0 / total
         p_edge = w_edge * inv
-        out = jnp.dot(jnp.where(causal, p_edge, 0.0).astype(BF16), kv[0, k, :, 256:384],
-                      preferred_element_type=F32)
-        out += jnp.dot(jnp.where(causal, 0.0, p_edge).astype(BF16), kv[4, k, :, 256:384],
-                       preferred_element_type=F32)
-        for slot in (1, 2, 3):
-            out += jnp.dot((w_inner[slot - 1] * inv).astype(BF16), kv[slot, k, :, 256:384],
-                           preferred_element_type=F32)
-        out_ref[:, pl.ds(pl.multiple_of(h * 128, 128), 128)] = out.astype(BF16)
-
-    def attend(group):
-        def body(i, _):
-            h = group * per * 2 + i
-            query_head(h, h // 2)
+        out = attend_to(jnp.where(causal, p_edge, 0.0), 4)
+        out += attend_to(jnp.where(causal, 0.0, p_edge), 0)
+        for m in inner:
+            out += attend_to(w_inner[m] * inv, m)
+        keep[...] = out.astype(BF16)
+
+    def columns(g):
+        return out_ref.at[:, pl.ds(pl.multiple_of((8 * zlo + 2 * g) * 128, 256), 256)]
+
+    def give(g):
+        return remote(result.at[1, g], columns(g), out_send.at[g], out_recv.at[g], pair)
+
+    def keep_own(g):
+        return pltpu.make_async_copy(result.at[0, g], columns(g), local_sem.at[5 + g])
+
+    def attend(g):
+        query_pair(g).wait_recv()
+        when(run >= 1, next_run(g, 1).wait_recv)
+        when(run >= 2, second_run(g).wait_recv)
+        when(run >= 2, from_relay(g).wait_recv)
+
+        def theirs(i, _):
+            query_head(g, 1 - zlo, q_in[2 * g + i],
+                       result.at[1, g, :, pl.ds(pl.multiple_of(i * 128, 128), 128)])
             return 0
 
-        lax.fori_loop(0, 2 * per, body, 0)
-
-    for g in (0, 1):
-        send(0, g)
-        send(2, g)
-    for g in range(groups):
-        receive(2, g)
-        send(1, g)
-        send(3, g)
-        send(4, g)
-        if g + 2 < groups:
-            send(0, g + 2)
-            send(2, g + 2)
-        receive(4, g)
-        send(5, g)
-        if g >= 1:
-            receive(1, g - 1)
-            receive(3, g - 1)
-            attend(g - 1)
-    receive(1, groups - 1)
-    receive(3, groups - 1)
-    attend(groups - 1)
-    for which in range(len(sends)):
-        for g in range(groups):
-            drain(which, g)
+        def ours(i, _):
+            query_head(g, zlo, q_own[8 * zlo + 2 * g + i],
+                       result.at[0, g, :, pl.ds(pl.multiple_of(i * 128, 128), 128)])
+            return 0
+
+        lax.fori_loop(0, 2, theirs, 0)
+        give(g).start()
+        lax.fori_loop(0, 2, ours, 0)
+        keep_own(g).start()
+
+    hop(0)
+    hop(1)
+    forward(0)
+    send_own(2)
+    hop(2)
+    forward(1)
+    send_own(3)
+    attend(0)
+    hop(3)
+    forward(2)
+    attend(1)
+    forward(3)
+    attend(2)
+    attend(3)
+
+    for copy in sent:
+        copy.wait_send()
+
+    def drain(h, _):
+        part(h).wait_send()
+        return 0
+
+    lax.fori_loop(0, 16, drain, 0)
+    for g in range(4):
+        over_pair(g).wait_send()
+        query_pair(g).wait_send()
+        when(has_next, next_run(g, 0).wait_send)
+        when(has_next, next_run(g, 1).wait_send)
+        when((run >= 1) & has_next, second_run(g).wait_send)
+        when(has_second, to_relay(g).wait_send)
+        when(relays, from_relay(g).wait_send)
+        keep_own(g).wait()
+        give(g).wait()
 
 
 def on_device(tokens, norm_gain, w_query, w_keyval, q_gain, k_gain):
@@ -438,40 +468,32 @@
     anyspace = pl.BlockSpec(memory_space=pl.ANY)
     dma = pltpu.SemaphoreType.DMA
     block = pltpu.VMEM((4, 4, 4, third, 128), BF16)
-    q, kv = pl.pallas_call(
-        project_kernel,
-        name="project",
-        out_shape=(
-            jax.ShapeDtypeStruct((heads, rows, 256), BF16),
-            jax.ShapeDtypeStruct((heads // 2, rows, 384), BF16),
-        ),
+    out = pl.pallas_call(
+        layer_kernel,
+        name="layer",
+        out_shape=jax.ShapeDtypeStruct((rows, heads * 128), BF16),
         in_specs=[vmem, vmem, anyspace, vmem, vmem, vmem, vmem],
-        out_specs=(vmem, vmem),
+        out_specs=vmem,
         scratch_shapes=[
             block, block, block,
             pltpu.VMEM((4, 3, rows, third), BF16),
             pltpu.VMEM((2, 2, 3, rows, third), BF16),
             pltpu.VMEM((heads, 2, rows, 256), F32),
             pltpu.VMEM((heads, rows, 256), F32),
-            dma((5,)), dma((3, 3, 2, 2)), dma((3, 3, 2, 2)),
+            pltpu.VMEM((heads, rows, 256), BF16),
+            pltpu.VMEM((heads // 2, rows, 256), BF16),
+            pltpu.VMEM((4, rows, 384), BF16),
+            pltpu.VMEM((4, 6, rows, 384), BF16),
+            pltpu.VMEM((4, rows, 384), BF16),
+            pltpu.VMEM((2, 4, rows, 256), BF16),
+            dma((9,)), dma((3, 3, 2, 2)), dma((3, 3, 2, 2)),
             dma((2,)), dma((2,)), dma((heads,)), dma((heads,)),
+            dma((2, 4)), dma((2, 4)), dma((5, 4)), dma((4, 4)), dma((4,)),
+            dma((4,)), dma((4,)),
         ],
         compiler_params=pltpu.CompilerParams(
-            collective_id=0, has_side_effects=True, vmem_limit_bytes=63 * 2**20),
+            collective_id=0, has_side_effects=True, vmem_limit_bytes=67043328),
     )(tokens[0], norm_gain[None], shard, cos, sin, ga, gb)
-    out = pl.pallas_call(
-        attend_kernel,
-        name="attend",
-        out_shape=jax.ShapeDtypeStruct((rows, heads * 128), BF16),
-        in_specs=[vmem, anyspace],
-        out_specs=vmem,
-        scratch_shapes=[
-            pltpu.VMEM((5, heads // 2, rows, 384), BF16),
-            dma, dma((5, 4)), dma((5, 4)),
-        ],
-        compiler_params=pltpu.CompilerParams(
-            collective_id=1, has_side_effects=True, vmem_limit_bytes=48 * 2**20),
-    )(q, kv)
     return out[None]
 
 

time: 212 us -> 190 us (0.90); the launches traced: 209 us -> 190 us
  Pallas kernels: 198 us -> 180 us
    pallas_call x2 -> x1, Pallas kernels: 198 us -> 180 us  [on_device(): pl.pallas_call(layer_kernel, name='layer', out_shape=jax.ShapeDtypeStruct...]
where the time goes in v2:
time: 190 us
  Pallas kernels  180 us (95%)
  local copies, waits for them, and re-layouts  7.67 us (4%)
  other arithmetic  2.01 us (1%)
    pallas_call x1, Pallas kernels, on_device(): pl.pallas_call(layer_kernel, name='layer', out_shape=jax.ShapeDtypeStruct...  180 us

profile of v2, /device:TPU:8, one launch (start us, length us, event | category | flops | bytes accessed | tf_op | source)
XLA Modules:
  0.0 190.1 jit_solution(17589401688434439191)
XLA Ops:
  0.0 0.8 fusion
  0.8 0.8 fusion.1
  1.6 0.7 maximum_bitcast_fusion
  2.3 1.4 broadcast_in_dim.14.gain_ref
  3.6 0.3 multiply_sine_fusion
  4.0 0.7 copy.10.sin_ref
  4.7 0.7 copy.9.cos_ref
  5.5 1.0 pad_maximum_fusion
  6.5 0.9 copy.8
  7.4 180.4 %layer.1 = bf16[256,2048]{1,0:T(8,128)(2,1)} custom-call(bf16[256,5376]{1,0:T(8,128)(2,1)} %bitcast.10, f32[1,5376]{1,0:T(1,128)} %broadcast_in_dim.14.gain_ref, bf16[3,448,128]{2,1,0:T(8,128)(2,1)} %bitcast.11, f32[256,128]{1,0:T(8,128)} %copy.9.cos_ref, f32[256,128]{1,0:T(8,128)} %copy.10.sin_ref, f32[1,128]{1,0:T(1,128)} %get-tuple-element.11.ga_ref, ...), custom_call_target="tpu_custom_call" | custom-call | tf_op jit(solution)/shard_map/layer/pallas_call | solution.py:471
  187.8 2.3 %copy.12 = bf16[1,256,2048]{2,1,0:T(8,128)(2,1)} copy(bf16[1,256,2048]{2,1,0:T(8,128)(2,1)} %bitcast.9) | data formatting | bytes 2097152
  (4 shorter events, 0.0 us)

commit v3 on v2

v3 whole, which is shorter than its diff:
```python
import functools
import math

import jax
import jax.numpy as jnp
from jax import lax
from jax.experimental import pallas as pl
from jax.experimental.pallas import tpu as pltpu
from jax.sharding import PartitionSpec as P

WINDOW = 1024
QSCALE = 168
MESH = pl.DeviceIdType.MESH
F32 = jnp.float32
BF16 = jnp.bfloat16
NEG = -1e30

WIDTHS = (512, 512, 320)
STARTS = (0, 512, 1024)
ORDERS = {
    "kv": (("x", "y", "z"), ("y", "z", "x"), ("z", "x", "y")),
    "q": (("x", "z", "y"), ("x", "y", "z"), ("x", "z", "y")),
}


def position():
    f, s = lax.axis_index("fsdp"), lax.axis_index("seq")
    return {"x": (s // 2) % 4, "y": s // 8, "z": 2 * (f // 2) + s % 2}, f % 2


def device(at, core):
    return (2 * (at["z"] // 2) + core, 8 * at["y"] + 2 * at["x"] + at["z"] % 2)


def shifted(at, dim, by):
    moved = dict(at)
    moved[dim] = (at[dim] + by + 4) % 4
    return moved


def layer_kernel(
    tok_hbm, gain_ref, wq_ref, wkv_ref, cos_hbm, sin_hbm, qg_ref, kg_ref,
    out_ref,
    kv0, kv1, kv2, q0, q1, q2, tok, cos_ref, sin_ref,
    normed, spread, acc, other, q_own, q_in, kv_out, kv, relay, result,
    local_sem, ring_send, ring_recv, tok_send, tok_recv, part_send, part_recv,
    pair_send, pair_recv, x_send, x_recv, relay_recv, out_send, out_recv,
):
    at, core = position()
    partner = device(at, 1 - core)
    rows, quarter = tok.shape[0], wq_ref.shape[1]
    weights = {"kv": (kv0, kv1, kv2), "q": (q0, q1, q2)}
    shards = {"kv": wkv_ref, "q": wq_ref}
    kinds = ("kv", "q")
    f, s = lax.axis_index("fsdp"), lax.axis_index("seq")
    zlo = s % 2
    run = s // 2
    runs = 16

    relayed = 4 * at["y"] + (at["x"] + 1) % 4
    relay_to = (f, 2 * ((relayed + 2) % runs) + zlo)
    relay_by = device(shifted(at, "x", -1), core)
    ahead = (f, (s + 2) % (2 * runs))
    behind = (f, (s - 2 + 2 * runs) % (2 * runs))
    pair = (f, s + 1 - 2 * zlo)
    source = (run - 2 + runs) % runs
    relay_from = (f, 2 * (4 * (source // 4) + (source + 3) % 4) + zlo)

    barrier = pltpu.get_barrier_semaphore()
    peers = [device(shifted(at, d, by), core) for d in "xyz" for by in (1, -1)]
    peers += [partner, ahead, behind, relay_to, relay_from]
    for peer in peers:
        pl.semaphore_signal(barrier, inc=1, device_id=peer, device_id_type=MESH)

    def clear(first, absent):
        @pl.when(absent)
        def _():
            kv[:, first:first + 2] = jnp.zeros((4, 2) + kv.shape[2:], BF16)

    clear(0, run < 2)
    clear(2, run < 1)

    fetched = [
        pltpu.make_async_copy(tok_hbm, tok, local_sem.at[9]),
        pltpu.make_async_copy(cos_hbm, cos_ref, local_sem.at[10]),
        pltpu.make_async_copy(sin_hbm, sin_ref, local_sem.at[11]),
    ]
    for copy in fetched:
        copy.start()
    for kind in kinds:
        for c, (d1, d2, d3) in enumerate(ORDERS[kind]):
            weights[kind][c][at[d3], at[d2], at[d1]] = (
                shards[kind][:, STARTS[c]:STARTS[c] + WIDTHS[c]])
    pl.semaphore_wait(barrier, len(peers))

    sent = []

    def view(kind, c, phase, index, half):
        d1, d2, d3 = ORDERS[kind][c]
        w = weights[kind][c]
        if phase == 0:
            if half is None:
                return w.at[at[d3], at[d2], index]
            return w.at[at[d3], at[d2], index, pl.ds(32 * half, 32)]
        if phase == 1:
            if half is None:
                return w.at[at[d3], index]
            return w.at[at[d3], index, pl.ds(2 * half, 2)]
        if half is None:
            return w.at[index]
        return w.at[index, pl.ds(2 * half, 2)]

    def ring(kind, c, phase, step):
        dim = ORDERS[kind][c][phase]
        copies = []
        for side, by in enumerate((1, -1)):
            if step == 0:
                block = view(kind, c, phase, at[dim], None)
            else:
                block = view(kind, c, phase, shifted(at, dim, -by)[dim], side)
            where = (kinds.index(kind), c, phase, step, side)
            copies.append(pltpu.make_async_remote_copy(
                src_ref=block, dst_ref=block,
                send_sem=ring_send.at[where], recv_sem=ring_recv.at[where],
                device_id=device(shifted(at, dim, by), core), device_id_type=MESH))
        return copies

    flying = {}

    def start_ring(kind, phase, step):
        flying[kind] = [ring(kind, c, phase, step) for c in range(3)]
        for copies in flying[kind]:
            for copy in copies:
                copy.start()
            sent.extend(copies)

    def wait_ring(kind):
        for copies in flying[kind]:
            for copy in copies:
                copy.wait_recv()

    start_ring("kv", 0, 0)
    wait_ring("kv")
    start_ring("kv", 0, 1)
    start_ring("q", 0, 0)
    wait_ring("kv")
    start_ring("kv", 1, 0)
    wait_ring("q")
    start_ring("q", 0, 1)
    wait_ring("kv")
    start_ring("kv", 1, 1)
    wait_ring("kv")
    start_ring("kv", 2, 0)
    wait_ring("q")

    strip = 32
    for copy in fetched:
        copy.wait()
    gain = jnp.concatenate([gain_ref[j:j + 1] for j in range(gain_ref.shape[0])], axis=1)

    def norm_rows(i, _):
        at_row = pl.ds(pl.multiple_of(i * strip, strip), strip)
        flat = tok[at_row, :].astype(F32)
        mean = jnp.mean(flat * flat, axis=-1, keepdims=True)
        out = (flat * lax.rsqrt(mean + 1e-6) * gain).astype(BF16)
        for k in range(4):
            normed[k, at_row, :] = out[:, k * quarter:(k + 1) * quarter]
        return 0

    lax.fori_loop(0, rows // strip, norm_rows, 0)
    exchange = []
    for zh in range(2):
        pltpu_copy = pltpu.make_async_copy(
            normed.at[2 * zh + core], spread.at[zh, core], local_sem.at[3 + zh])
        pltpu_copy.start()
        remote = pltpu.make_async_remote_copy(
            src_ref=normed.at[2 * zh + 1 - core], dst_ref=spread.at[zh, core],
            send_sem=tok_send.at[zh], recv_sem=tok_recv.at[zh],
            device_id=partner, device_id_type=MESH)
        remote.start()
        exchange.append((pltpu_copy, remote))
    for mine, remote in exchange:
        mine.wait()
        remote.wait()

    x, y, zown = at["x"], at["y"], at["z"] // 2
    zfar, mine_x = 1 - zown, x // 2
    far_y, far_x = (y + 2) % 4, 1 - mine_x

    def weight(kind, c, z, yy, xx):
        index = {"x": xx, "y": yy, "z": z}
        d1, d2, d3 = ORDERS[kind][c]
        return weights[kind][c][index[d3], index[d2], index[d1]]

    def units(kind, yy, xp, parts, first):
        h = 8 * kinds.index(kind) + 2 * yy + xp
        total = None
        for c, zh in parts:
            rhs = jnp.concatenate(
                [weight(kind, c, 2 * zh + z, yy, 2 * xp + i) for i in (0, 1) for z in (0, 1)], axis=0)
            lhs = spread[zh, :, :, STARTS[c]:STARTS[c] + WIDTHS[c]].reshape(2 * rows, WIDTHS[c])
            term = lax.dot_general(lhs, rhs, (((1,), (1,)), ((), ())), preferred_element_type=F32)
            total = term if total is None else total + term
        total = total.reshape(2, rows, 256)
        if first:
            acc[h] = total
        else:
            acc[h] += total

    def part(h):
        return pltpu.make_async_remote_copy(
            src_ref=acc.at[h, 1 - core], dst_ref=other.at[h],
            send_sem=part_send.at[h], recv_sem=part_recv.at[h],
            device_id=partner, device_id_type=MESH)

    both = lambda c: [(c, 0), (c, 1)]

    def loop(n, body):
        def step(i, _):
            body(i)
            return 0
        lax.fori_loop(0, n, step, 0)

    def near(k):
        return (y + k + k // 2) % 4

    def early(kind, yy, xp, parts):
        units(kind, yy, xp, parts, True)

    def late(kind, yy, xp, parts):
        units(kind, yy, xp, parts, False)
        part(8 * kinds.index(kind) + 2 * yy + xp).start()

    wait_ring("kv")
    start_ring("kv", 2, 1)
    start_ring("q", 1, 0)
    loop(3, lambda i: early("kv", near(i), mine_x, [(0, zown)] + both(1) + both(2)))
    early("kv", far_y, mine_x, [(0, zown)] + both(1))
    loop(3, lambda i: early("kv", near(i), far_x, [(0, zown)] + both(2)))
    early("kv", far_y, far_x, [(0, zown)])
    wait_ring("kv")
    loop(3, lambda i: late("kv", near(i), mine_x, [(0, zfar)]))
    late("kv", far_y, mine_x, [(0, zfar)] + both(2))
    loop(3, lambda i: late("kv", near(i), far_x, [(0, zfar)] + both(1)))
    late("kv", far_y, far_x, [(0, zfar)] + both(1) + both(2))
    wait_ring("q")
    start_ring("q", 1, 1)

    def turned(values, gain):
        mean = jnp.mean(values * values, axis=-1, keepdims=True)
        values = values * lax.rsqrt(mean + 1e-6) * gain
        return values * cos_ref[...] + pltpu.roll(values, 64, 1) * sin_ref[...]

    def in_two(ref, values):
        high = values.astype(BF16)
        ref[:, 0:128] = high
        ref[:, 128:256] = (values - high.astype(F32)).astype(BF16)

    def summed(h, i):
        lanes = slice(128 * i, 128 * i + 128)
        return acc[h, core, :, lanes] + other[h, :, lanes]

    def remote(src, dst, send_sem, recv_sem, to):
        return pltpu.make_async_remote_copy(
            src_ref=src, dst_ref=dst, send_sem=send_sem, recv_sem=recv_sem,
            device_id=to, device_id_type=MESH)

    def over_pair(g):
        return remote(kv_out.at[g], kv.at[g, 4 + zlo], pair_send.at[0, g], pair_recv.at[0, g], pair)

    def query_pair(g):
        mine = pl.ds(8 * (1 - zlo) + 2 * g, 2)
        return remote(q_own.at[mine], q_in.at[pl.ds(2 * g, 2)],
                      pair_send.at[1, g], pair_recv.at[1, g], pair)

    def next_run(g, block):
        return remote(kv.at[g, 4 + block], kv.at[g, 2 + block],
                      x_send.at[block, g], x_recv.at[2 + block, g], ahead)

    def second_run(g):
        return remote(kv.at[g, 2], kv.at[g, 0], x_send.at[2, g], x_recv.at[0, g], ahead)

    def to_relay(g):
        return remote(kv.at[g, 5], relay.at[g], x_send.at[3, g], relay_recv.at[g], relay_by)

    def from_relay(g):
        return remote(relay.at[g], kv.at[g, 1], x_send.at[4, g], x_recv.at[1, g], relay_to)

    def when(condition, action):
        @pl.when(condition)
        def _():
            action()

    has_next, has_second = run + 1 < runs, run + 2 < runs
    relays = relayed + 2 < runs

    def send_own(g):
        when(has_next, next_run(g, zlo).start)
        when(has_second & (zlo == 1), to_relay(g).start)

    def hop(g):
        over_pair(g).wait_recv()
        when(has_next, next_run(g, 1 - zlo).start)
        when(has_second & (zlo == 0), to_relay(g).start)

    def forward(g):
        when(run >= 1, next_run(g, 0).wait_recv)
        when((run >= 1) & has_next, second_run(g).start)
        when(relays, to_relay(g).wait_recv)
        when(relays, from_relay(g).start)

    def key_values(j):
        for mine in (True, False):
            half = zlo if mine else 1 - zlo
            key_pair, value_pair = 2 * half + j, 4 + 2 * half + j
            part(key_pair).wait_recv()
            part(value_pair).wait_recv()
            for i in (0, 1):
                g = 2 * j + i
                keep = kv.at[g, 4 + zlo] if mine else kv_out.at[g]
                in_two(keep, turned(summed(key_pair, i), kg_ref[...]))
                keep[:, 256:384] = summed(value_pair, i).astype(BF16)
        over_pair(2 * j).start()
        over_pair(2 * j + 1).start()
        when(j == 0, lambda: send_own(0))
        when(j == 0, lambda: send_own(1))

    loop(2, key_values)
    wait_ring("q")
    start_ring("q", 2, 0)
    hop(0)
    hop(1)
    forward(0)
    send_own(2)
    hop(2)
    forward(1)
    send_own(3)
    hop(3)
    forward(2)
    wait_ring("q")
    start_ring("q", 2, 1)
    forward(3)

    loop(6, lambda i: early("q", near(i // 2), i % 2, [(1, zown)] + both(0) + both(2)))
    loop(2, lambda i: early("q", far_y, i, [(1, zown)]))
    wait_ring("q")
    loop(6, lambda i: late("q", near(i // 2), i % 2, [(1, zfar)]))
    loop(2, lambda i: late("q", far_y, i, [(1, zfar)] + both(0) + both(2)))

    query_gain = qg_ref[...] * (QSCALE ** -0.5 * math.log2(math.e))

    def queries(g, mine):
        head = 8 * (zlo if mine else 1 - zlo) + 2 * g
        pair_unit = 8 + head // 2
        part(pair_unit).wait_recv()
        for i in (0, 1):
            in_two(q_own.at[head + i], turned(summed(pair_unit, i), query_gain))

    def theirs_first(g):
        queries(g, False)
        query_pair(g).start()

    loop(4, theirs_first)
    loop(4, lambda g: queries(g, True))

    row = lax.broadcasted_iota(jnp.int32, (2 * rows, rows), 0) % rows
    col = lax.broadcasted_iota(jnp.int32, (2 * rows, rows), 1)
    causal = col <= row

    def two_heads(g, token_block, q, keep):
        q = q.reshape(2 * rows, 256)
        q_hi, q_lo = q[:, 0:128], q[:, 128:256]
        q = jnp.concatenate([q_hi, q_hi, q_lo, q_lo], axis=1)
        pen = [jnp.where(2 * run - 4 + token_block + m >= 0, 0.0, NEG).astype(F32)
               for m in range(5)]

        def score(m):
            keys = kv[g, token_block + m, :, 0:256]
            keys = jnp.concatenate([keys, keys], axis=1)
            return lax.dot_general(q, keys, (((1,), (1,)), ((), ())), preferred_element_type=F32)

        edge = jnp.where(causal, score(4), score(0) + pen[0])
        inner = {m: score(m) for m in (1, 2, 3)}
        top = jnp.max(edge, axis=-1, keepdims=True)
        for m in inner:
            top = jnp.maximum(top, jnp.max(inner[m], axis=-1, keepdims=True) + pen[m])
        w_edge = jnp.exp2(edge - top)
        w_inner = {m: jnp.exp2(inner[m] - (top - pen[m])) for m in inner}
        total = jnp.sum(w_edge, axis=-1, keepdims=True)
        for m in inner:
            total = total + jnp.sum(w_inner[m], axis=-1, keepdims=True)
        inv = 1.0 / total
        p_edge = w_edge * inv
        probs = [jnp.where(causal, 0.0, p_edge)] + [w_inner[m] * inv for m in inner]
        probs.append(jnp.where(causal, p_edge, 0.0))
        probs = jnp.concatenate([p.astype(BF16) for p in probs], axis=1)
        values = kv[g, pl.ds(token_block, 5), :, 256:384].reshape(5 * rows, 128)
        out = jnp.dot(probs, values, preferred_element_type=F32).astype(BF16)
        keep[:, 0:128] = out[:rows]
        keep[:, 128:256] = out[rows:]

    def columns(g):
        return out_ref.at[:, pl.ds(pl.multiple_of((8 * zlo + 2 * g) * 128, 256), 256)]

    def give(g):
        return remote(result.at[1, g], columns(g), out_send.at[g], out_recv.at[g], pair)

    def keep_own(g):
        return pltpu.make_async_copy(result.at[0, g], columns(g), local_sem.at[5 + g])

    def mine_of(g):
        when(run >= 1, next_run(g, 1).wait_recv)
        when(run >= 2, second_run(g).wait_recv)
        when(run >= 2, from_relay(g).wait_recv)
        two_heads(g, zlo, q_own[pl.ds(8 * zlo + 2 * g, 2)], result.at[0, g])
        keep_own(g).start()

    def theirs_of(g):
        query_pair(g).wait_recv()
        two_heads(g, 1 - zlo, q_in[pl.ds(2 * g, 2)], result.at[1, g])
        give(g).start()

    loop(4, mine_of)
    loop(4, theirs_of)

    for copy in sent:
        copy.wait_send()

    def drain(h, _):
        part(h).wait_send()
        return 0

    lax.fori_loop(0, 16, drain, 0)
    for g in range(4):
        over_pair(g).wait_send()
        query_pair(g).wait_send()
        when(has_next, next_run(g, 0).wait_send)
        when(has_next, next_run(g, 1).wait_send)
        when((run >= 1) & has_next, second_run(g).wait_send)
        when(has_second, to_relay(g).wait_send)
        when(relays, from_relay(g).wait_send)
        keep_own(g).wait()
        give(g).wait()


def on_device(tokens, norm_gain, w_query, w_keyval, q_gain, k_gain):
    rows, width = tokens.shape[1:]
    quarter, cols = w_query.shape
    heads = cols * lax.axis_size("seq") // q_gain.shape[0]
    half = q_gain.shape[0] // 2
    place = (lax.axis_index("seq") * rows + jnp.arange(rows)).astype(F32)
    freq = jnp.power(10000.0, -2.0 * (jnp.arange(2 * half) % half).astype(F32) / (2 * half))
    angle = place[:, None] * freq[None, :]
    cos = jnp.cos(angle)
    sin = jnp.where(jnp.arange(2 * half) < half, -1.0, 1.0) * jnp.sin(angle)
    vmem = pl.BlockSpec(memory_space=pltpu.VMEM)
    anyspace = pl.BlockSpec(memory_space=pl.ANY)
    dma = pltpu.SemaphoreType.DMA
    blocks = [pltpu.VMEM((4, 4, 4, cols, width), BF16) for width in WIDTHS]
    out = pl.pallas_call(
        layer_kernel,
        name="layer",
        out_shape=jax.ShapeDtypeStruct((rows, heads * 128), BF16),
        in_specs=[anyspace, vmem, vmem, vmem, anyspace, anyspace, vmem, vmem],
        out_specs=vmem,
        scratch_shapes=[
            *blocks, *blocks,
            pltpu.VMEM((rows, width), BF16),
            pltpu.VMEM((rows, 128), F32),
            pltpu.VMEM((rows, 128), F32),
            pltpu.VMEM((4, rows, quarter), BF16),
            pltpu.VMEM((2, 2, rows, quarter), BF16),
            pltpu.VMEM((heads, 2, rows, 256), F32),
            pltpu.VMEM((heads, rows, 256), F32),
            pltpu.VMEM((heads, rows, 256), BF16),
            pltpu.VMEM((heads // 2, rows, 256), BF16),
            pltpu.VMEM((4, rows, 384), BF16),
            pltpu.VMEM((4, 6, rows, 384), BF16),
            pltpu.VMEM((4, rows, 384), BF16),
            pltpu.VMEM((2, 4, rows, 256), BF16),
            dma((12,)), dma((2, 3, 3, 2, 2)), dma((2, 3, 3, 2, 2)),
            dma((2,)), dma((2,)), dma((heads,)), dma((heads,)),
            dma((2, 4)), dma((2, 4)), dma((5, 4)), dma((4, 4)), dma((4,)),
            dma((4,)), dma((4,)),
        ],
        compiler_params=pltpu.CompilerParams(
            collective_id=0, has_side_effects=True, vmem_limit_bytes=67043328),
    )(tokens[0], norm_gain.reshape(-1, 128), w_query.T, w_keyval.T, cos, sin,
      q_gain[None], k_gain[None])
    return out[None]


def solution(mesh):
    in_specs = (P("fsdp", "seq", None), P(), P("fsdp", "seq"), P("fsdp", "seq"), P(), P())
    out_specs = P("fsdp", "seq", None)
    return jax.shard_map(
        on_device, mesh=mesh, in_specs=in_specs, out_specs=out_specs, check_vma=False
    )
```

time: 190 us -> 251 us (1.32); the launches traced: 190 us -> 247 us
  Pallas kernels: 180 us -> 244 us
  local copies, waits for them, and re-layouts: 7.67 us -> 2.3 us
    pallas_call x1, Pallas kernels: 180 us -> 244 us  [on_device(): pl.pallas_call(layer_kernel, name='layer', out_shape=jax.ShapeDtypeStruct...]
where the time goes in v3:
time: 251 us; the launch traced here: 247 us
  Pallas kernels  244 us (97%)
    pallas_call x1, Pallas kernels, on_device(): pl.pallas_call(layer_kernel, name='layer', out_shape=jax.ShapeDtypeStruct...  244 us

profile of v3, /device:TPU:8, one launch (start us, length us, event | category | flops | bytes accessed | tf_op | source)
XLA Modules:
  0.0 247.1 jit_solution(15578911086904535966)
XLA Ops:
  0.0 1.2 fusion
  1.3 243.5 %layer.1 = bf16[256,2048]{1,0:T(8,128)(2,1)} custom-call(bf16[256,5376]{1,0:T(8,128)(2,1)} %bitcast.8, f32[42,128]{1,0:T(8,128)} %bitcast.11, bf16[64,1344]{1,0:T(8,128)(2,1)} %bitcast.9, bf16[64,1344]{1,0:T(8,128)(2,1)} %bitcast.10, f32[256,128]{1,0:T(8,128)} %get-tuple-element.6.cos_hbm, f32[256,128]{1,0:T(8,128)} %get-tuple-element.5.sin_hbm, ...), custom_call_target="tpu_custom_call" | custom-call | tf_op jit(solution)/shard_map/layer/pallas_call | solution.py:460
  244.8 2.3 copy.8
  (2 shorter events, 0.0 us)

commit v4 on v3

--- a/solution.py
+++ b/solution.py
@@ -15,12 +15,7 @@
 BF16 = jnp.bfloat16
 NEG = -1e30
 
-WIDTHS = (512, 512, 320)
-STARTS = (0, 512, 1024)
-ORDERS = {
-    "kv": (("x", "y", "z"), ("y", "z", "x"), ("z", "x", "y")),
-    "q": (("x", "z", "y"), ("x", "y", "z"), ("x", "z", "y")),
-}
+ORDERS = (("x", "y", "z"), ("y", "z", "x"), ("z", "x", "y"))
 
 
 def position():
@@ -39,19 +34,17 @@
 
 
 def layer_kernel(
-    tok_hbm, gain_ref, wq_ref, wkv_ref, cos_hbm, sin_hbm, qg_ref, kg_ref,
+    tok_hbm, gain_ref, shard_hbm, cos_hbm, sin_hbm, qg_ref, kg_ref,
     out_ref,
-    kv0, kv1, kv2, q0, q1, q2, tok, cos_ref, sin_ref,
+    w0, w1, w2, tok, cos_ref, sin_ref,
     normed, spread, acc, other, q_own, q_in, kv_out, kv, relay, result,
     local_sem, ring_send, ring_recv, tok_send, tok_recv, part_send, part_recv,
     pair_send, pair_recv, x_send, x_recv, relay_recv, out_send, out_recv,
 ):
     at, core = position()
     partner = device(at, 1 - core)
-    rows, quarter = tok.shape[0], wq_ref.shape[1]
-    weights = {"kv": (kv0, kv1, kv2), "q": (q0, q1, q2)}
-    shards = {"kv": wkv_ref, "q": wq_ref}
-    kinds = ("kv", "q")
+    rows, third = tok.shape[0], w0.shape[3]
+    weights = (w0, w1, w2)
     f, s = lax.axis_index("fsdp"), lax.axis_index("seq")
     zlo = s % 2
     run = s // 2
@@ -87,21 +80,24 @@
     ]
     for copy in fetched:
         copy.start()
-    for kind in kinds:
-        for c, (d1, d2, d3) in enumerate(ORDERS[kind]):
-            weights[kind][c][at[d3], at[d2], at[d1]] = (
-                shards[kind][:, STARTS[c]:STARTS[c] + WIDTHS[c]])
+    own = []
+    for c, (d1, d2, d3) in enumerate(ORDERS):
+        own.append(pltpu.make_async_copy(
+            shard_hbm.at[c], weights[c].at[at[d3], at[d2], at[d1]], local_sem.at[c]))
+        own[-1].start()
+    for copy in own:
+        copy.wait()
     pl.semaphore_wait(barrier, len(peers))
 
     sent = []
 
-    def view(kind, c, phase, index, half):
-        d1, d2, d3 = ORDERS[kind][c]
-        w = weights[kind][c]
+    def view(c, phase, index, half):
+        d1, d2, d3 = ORDERS[c]
+        w = weights[c]
         if phase == 0:
             if half is None:
                 return w.at[at[d3], at[d2], index]
-            return w.at[at[d3], at[d2], index, pl.ds(32 * half, 32)]
+            return w.at[at[d3], at[d2], index, pl.ds(half * (third // 2), third // 2)]
         if phase == 1:
             if half is None:
                 return w.at[at[d3], index]
@@ -110,48 +106,39 @@
             return w.at[index]
         return w.at[index, pl.ds(2 * half, 2)]
 
-    def ring(kind, c, phase, step):
-        dim = ORDERS[kind][c][phase]
+    def ring(c, phase, step):
+        dim = ORDERS[c][phase]
         copies = []
         for side, by in enumerate((1, -1)):
             if step == 0:
-                block = view(kind, c, phase, at[dim], None)
+                block = view(c, phase, at[dim], None)
             else:
-                block = view(kind, c, phase, shifted(at, dim, -by)[dim], side)
-            where = (kinds.index(kind), c, phase, step, side)
+                block = view(c, phase, shifted(at, dim, -by)[dim], side)
             copies.append(pltpu.make_async_remote_copy(
                 src_ref=block, dst_ref=block,
-                send_sem=ring_send.at[where], recv_sem=ring_recv.at[where],
+                send_sem=ring_send.at[c, phase, step, side],
+                recv_sem=ring_recv.at[c, phase, step, side],
                 device_id=device(shifted(at, dim, by), core), device_id_type=MESH))
         return copies
 
-    flying = {}
-
-    def start_ring(kind, phase, step):
-        flying[kind] = [ring(kind, c, phase, step) for c in range(3)]
-        for copies in flying[kind]:
-            for copy in copies:
-                copy.start()
-            sent.extend(copies)
-
-    def wait_ring(kind):
-        for copies in flying[kind]:
-            for copy in copies:
+    def start(copies):
+        for copy in copies:
+            copy.start()
+        sent.extend(copies)
+
+    flying = [ring(c, 0, 0) for c in range(3)]
+    for copies in flying:
+        start(copies)
+
+    def step_ring(phase, step):
+        for c in range(3):
+            for copy in flying[c]:
                 copy.wait_recv()
-
-    start_ring("kv", 0, 0)
-    wait_ring("kv")
-    start_ring("kv", 0, 1)
-    start_ring("q", 0, 0)
-    wait_ring("kv")
-    start_ring("kv", 1, 0)
-    wait_ring("q")
-    start_ring("q", 0, 1)
-    wait_ring("kv")
-    start_ring("kv", 1, 1)
-    wait_ring("kv")
-    start_ring("kv", 2, 0)
-    wait_ring("q")
+            flying[c] = ring(c, phase, step)
+            start(flying[c])
+
+    for phase, step in ((0, 1), (1, 0), (1, 1), (2, 0)):
+        step_ring(phase, step)
 
     strip = 32
     for copy in fetched:
@@ -164,7 +151,9 @@
         mean = jnp.mean(flat * flat, axis=-1, keepdims=True)
         out = (flat * lax.rsqrt(mean + 1e-6) * gain).astype(BF16)
         for k in range(4):
-            normed[k, at_row, :] = out[:, k * quarter:(k + 1) * quarter]
+            for c in range(3):
+                j = 3 * k + c
+                normed[k, c, at_row, :] = out[:, j * third:(j + 1) * third]
         return 0
 
     lax.fori_loop(0, rows // strip, norm_rows, 0)
@@ -184,22 +173,21 @@
         remote.wait()
 
     x, y, zown = at["x"], at["y"], at["z"] // 2
-    zfar, mine_x = 1 - zown, x // 2
-    far_y, far_x = (y + 2) % 4, 1 - mine_x
-
-    def weight(kind, c, z, yy, xx):
+    zfar, far_x, far_y = 1 - zown, (x + 2) % 4, (y + 2) % 4
+
+    def weight(c, z, yy, xx):
         index = {"x": xx, "y": yy, "z": z}
-        d1, d2, d3 = ORDERS[kind][c]
-        return weights[kind][c][index[d3], index[d2], index[d1]]
-
-    def units(kind, yy, xp, parts, first):
-        h = 8 * kinds.index(kind) + 2 * yy + xp
+        d1, d2, d3 = ORDERS[c]
+        return weights[c][index[d3], index[d2], index[d1]]
+
+    def units(yy, xx, parts, first):
+        h = 4 * yy + xx
         total = None
         for c, zh in parts:
             rhs = jnp.concatenate(
-                [weight(kind, c, 2 * zh + z, yy, 2 * xp + i) for i in (0, 1) for z in (0, 1)], axis=0)
-            lhs = spread[zh, :, :, STARTS[c]:STARTS[c] + WIDTHS[c]].reshape(2 * rows, WIDTHS[c])
-            term = lax.dot_general(lhs, rhs, (((1,), (1,)), ((), ())), preferred_element_type=F32)
+                [weight(c, 2 * zh, yy, xx), weight(c, 2 * zh + 1, yy, xx)], axis=1)
+            term = jnp.dot(spread[zh, :, c].reshape(2 * rows, third), rhs,
+                           preferred_element_type=F32)
             total = term if total is None else total + term
         total = total.reshape(2, rows, 256)
         if first:
@@ -221,30 +209,32 @@
             return 0
         lax.fori_loop(0, n, step, 0)
 
-    def near(k):
-        return (y + k + k // 2) % 4
-
-    def early(kind, yy, xp, parts):
-        units(kind, yy, xp, parts, True)
-
-    def late(kind, yy, xp, parts):
-        units(kind, yy, xp, parts, False)
-        part(8 * kinds.index(kind) + 2 * yy + xp).start()
-
-    wait_ring("kv")
-    start_ring("kv", 2, 1)
-    start_ring("q", 1, 0)
-    loop(3, lambda i: early("kv", near(i), mine_x, [(0, zown)] + both(1) + both(2)))
-    early("kv", far_y, mine_x, [(0, zown)] + both(1))
-    loop(3, lambda i: early("kv", near(i), far_x, [(0, zown)] + both(2)))
-    early("kv", far_y, far_x, [(0, zown)])
-    wait_ring("kv")
-    loop(3, lambda i: late("kv", near(i), mine_x, [(0, zfar)]))
-    late("kv", far_y, mine_x, [(0, zfar)] + both(2))
-    loop(3, lambda i: late("kv", near(i), far_x, [(0, zfar)] + both(1)))
-    late("kv", far_y, far_x, [(0, zfar)] + both(1) + both(2))
-    wait_ring("q")
-    start_ring("q", 1, 1)
+    def near(at_dim, k):
+        return (at_dim + k + k // 2) % 4
+
+    def late(yy, xx, parts):
+        units(yy, xx, parts, False)
+        part(4 * yy + xx).start()
+
+    step_ring(2, 1)
+    loop(9, lambda i: units(near(y, i // 3), near(x, i % 3), [(0, zown)] + both(1) + both(2), True))
+    loop(3, lambda i: units(near(y, i), far_x, [(0, zown)] + both(2), True))
+    loop(3, lambda i: units(far_y, near(x, i), [(0, zown)] + both(1), True))
+    units(far_y, far_x, [(0, zown)], True)
+    for copies in flying:
+        for copy in copies:
+            copy.wait_recv()
+
+    def late_group(g):
+        @pl.when(g != far_x)
+        def _():
+            loop(3, lambda i: late(near(y, i), g, [(0, zfar)]))
+            late(far_y, g, [(0, zfar)] + both(2))
+
+        @pl.when(g == far_x)
+        def _():
+            loop(3, lambda i: late(near(y, i), g, [(0, zfar)] + both(1)))
+            late(far_y, g, [(0, zfar)] + both(1) + both(2))
 
     def turned(values, gain):
         mean = jnp.mean(values * values, axis=-1, keepdims=True)
@@ -256,9 +246,14 @@
         ref[:, 0:128] = high
         ref[:, 128:256] = (values - high.astype(F32)).astype(BF16)
 
-    def summed(h, i):
-        lanes = slice(128 * i, 128 * i + 128)
-        return acc[h, core, :, lanes] + other[h, :, lanes]
+    low = lax.broadcasted_iota(jnp.int32, (rows, 128), 1) < 64
+
+    def summed(h, is_query):
+        first = acc[h, core, :, 0:128] + other[h, :, 0:128]
+        second = acc[h, core, :, 128:256] + other[h, :, 128:256]
+        if is_query:
+            return jnp.where(low, first, pltpu.roll(second, 64, 1))
+        return jnp.where(low, pltpu.roll(first, 64, 1), second)
 
     def remote(src, dst, send_sem, recv_sem, to):
         return pltpu.make_async_remote_copy(
@@ -309,58 +304,40 @@
         when(relays, to_relay(g).wait_recv)
         when(relays, from_relay(g).start)
 
-    def key_values(j):
+    def key_values(g):
         for mine in (True, False):
-            half = zlo if mine else 1 - zlo
-            key_pair, value_pair = 2 * half + j, 4 + 2 * half + j
-            part(key_pair).wait_recv()
-            part(value_pair).wait_recv()
-            for i in (0, 1):
-                g = 2 * j + i
-                keep = kv.at[g, 4 + zlo] if mine else kv_out.at[g]
-                in_two(keep, turned(summed(key_pair, i), kg_ref[...]))
-                keep[:, 256:384] = summed(value_pair, i).astype(BF16)
-        over_pair(2 * j).start()
-        over_pair(2 * j + 1).start()
-        when(j == 0, lambda: send_own(0))
-        when(j == 0, lambda: send_own(1))
-
-    loop(2, key_values)
-    wait_ring("q")
-    start_ring("q", 2, 0)
+            k = 4 * (zlo if mine else 1 - zlo) + g
+            keep = kv.at[g, 4 + zlo] if mine else kv_out.at[g]
+            part(k).wait_recv()
+            part(8 + k).wait_recv()
+            in_two(keep, turned(summed(k, False), kg_ref[...]))
+            keep[:, 256:384] = summed(8 + k, False).astype(BF16)
+        over_pair(g).start()
+        when(g < 2, lambda: send_own(g))
+
+    def stage(n):
+        when(n < 4, lambda: late_group(n))
+        when(n > 0, lambda: key_values(n - 1))
+
+    loop(5, stage)
+
+    query_gain = qg_ref[...] * (QSCALE ** -0.5 * math.log2(math.e))
+
+    def queries(g, mine):
+        head = 8 * (zlo if mine else 1 - zlo) + 2 * g
+        for i in (0, 1):
+            in_two(q_own.at[head + i], turned(summed(head + i, True), query_gain))
+
+    def queries_out(g):
+        queries(g, False)
+        query_pair(g).start()
+
     hop(0)
     hop(1)
+    loop(4, queries_out)
     forward(0)
     send_own(2)
     hop(2)
-    forward(1)
-    send_own(3)
-    hop(3)
-    forward(2)
-    wait_ring("q")
-    start_ring("q", 2, 1)
-    forward(3)
-
-    loop(6, lambda i: early("q", near(i // 2), i % 2, [(1, zown)] + both(0) + both(2)))
-    loop(2, lambda i: early("q", far_y, i, [(1, zown)]))
-    wait_ring("q")
-    loop(6, lambda i: late("q", near(i // 2), i % 2, [(1, zfar)]))
-    loop(2, lambda i: late("q", far_y, i, [(1, zfar)] + both(0) + both(2)))
-
-    query_gain = qg_ref[...] * (QSCALE ** -0.5 * math.log2(math.e))
-
-    def queries(g, mine):
-        head = 8 * (zlo if mine else 1 - zlo) + 2 * g
-        pair_unit = 8 + head // 2
-        part(pair_unit).wait_recv()
-        for i in (0, 1):
-            in_two(q_own.at[head + i], turned(summed(pair_unit, i), query_gain))
-
-    def theirs_first(g):
-        queries(g, False)
-        query_pair(g).start()
-
-    loop(4, theirs_first)
     loop(4, lambda g: queries(g, True))
 
     row = lax.broadcasted_iota(jnp.int32, (2 * rows, rows), 0) % rows
@@ -420,8 +397,19 @@
         two_heads(g, 1 - zlo, q_in[pl.ds(2 * g, 2)], result.at[1, g])
         give(g).start()
 
-    loop(4, mine_of)
-    loop(4, theirs_of)
+    def attend(g):
+        mine_of(g)
+        theirs_of(g)
+
+    forward(1)
+    send_own(3)
+    attend(0)
+    hop(3)
+    forward(2)
+    attend(1)
+    forward(3)
+    attend(2)
+    attend(3)
 
     for copy in sent:
         copy.wait_send()
@@ -448,6 +436,8 @@
     quarter, cols = w_query.shape
     heads = cols * lax.axis_size("seq") // q_gain.shape[0]
     half = q_gain.shape[0] // 2
+    third = quarter // 3
+    shard = jnp.concatenate([w_query, w_keyval], axis=1).reshape(3, third, 2 * cols)
     place = (lax.axis_index("seq") * rows + jnp.arange(rows)).astype(F32)
     freq = jnp.power(10000.0, -2.0 * (jnp.arange(2 * half) % half).astype(F32) / (2 * half))
     angle = place[:, None] * freq[None, :]
@@ -456,20 +446,20 @@
     vmem = pl.BlockSpec(memory_space=pltpu.VMEM)
     anyspace = pl.BlockSpec(memory_space=pl.ANY)
     dma = pltpu.SemaphoreType.DMA
-    blocks = [pltpu.VMEM((4, 4, 4, cols, width), BF16) for width in WIDTHS]
+    block = pltpu.VMEM((4, 4, 4, third, 128), BF16)
     out = pl.pallas_call(
         layer_kernel,
         name="layer",
         out_shape=jax.ShapeDtypeStruct((rows, heads * 128), BF16),
-        in_specs=[anyspace, vmem, vmem, vmem, anyspace, anyspace, vmem, vmem],
+        in_specs=[anyspace, vmem, anyspace, anyspace, anyspace, vmem, vmem],
         out_specs=vmem,
         scratch_shapes=[
-            *blocks, *blocks,
+            block, block, block,
             pltpu.VMEM((rows, width), BF16),
             pltpu.VMEM((rows, 128), F32),
             pltpu.VMEM((rows, 128), F32),
-            pltpu.VMEM((4, rows, quarter), BF16),
-            pltpu.VMEM((2, 2, rows, quarter), BF16),
+            pltpu.VMEM((4, 3, rows, third), BF16),
+            pltpu.VMEM((2, 2, 3, rows, third), BF16),
             pltpu.VMEM((heads, 2, rows, 256), F32),
             pltpu.VMEM((heads, rows, 256), F32),
             pltpu.VMEM((heads, rows, 256), BF16),
@@ -478,14 +468,14 @@
             pltpu.VMEM((4, 6, rows, 384), BF16),
             pltpu.VMEM((4, rows, 384), BF16),
             pltpu.VMEM((2, 4, rows, 256), BF16),
-            dma((12,)), dma((2, 3, 3, 2, 2)), dma((2, 3, 3, 2, 2)),
+            dma((12,)), dma((3, 3, 2, 2)), dma((3, 3, 2, 2)),
             dma((2,)), dma((2,)), dma((heads,)), dma((heads,)),
             dma((2, 4)), dma((2, 4)), dma((5, 4)), dma((4, 4)), dma((4,)),
             dma((4,)), dma((4,)),
         ],
         compiler_params=pltpu.CompilerParams(
             collective_id=0, has_side_effects=True, vmem_limit_bytes=67043328),
-    )(tokens[0], norm_gain.reshape(-1, 128), w_query.T, w_keyval.T, cos, sin,
+    )(tokens[0], norm_gain.reshape(-1, 128), shard, cos, sin,
       q_gain[None], k_gain[None])
     return out[None]
 

time: 251 us -> 183 us (0.73); the launches traced: 247 us -> 182 us
  Pallas kernels: 244 us -> 176 us
    pallas_call x1, Pallas kernels: 244 us -> 176 us  [on_device(): pl.pallas_call(layer_kernel, name='layer', out_shape=jax.ShapeDtypeStruct...]
where the time goes in v4:
time: 183 us; the launch traced here: 182 us
  Pallas kernels  176 us (96%)
  local copies, waits for them, and re-layouts  3.21 us (2%)
  other arithmetic  2.32 us (1%)
    pallas_call x1, Pallas kernels, on_device(): pl.pallas_call(layer_kernel, name='layer', out_shape=jax.ShapeDtypeStruct...  176 us

profile of v4, /device:TPU:8, one launch (start us, length us, event | category | flops | bytes accessed | tf_op | source)
XLA Modules:
  0.0 181.9 jit_solution(5709530680290145474)
XLA Ops:
  0.0 1.3 fusion
  1.3 1.0 pad_maximum_fusion
  2.3 0.9 copy.7
  3.2 176.4 %layer.1 = bf16[256,2048]{1,0:T(8,128)(2,1)} custom-call(bf16[256,5376]{1,0:T(8,128)(2,1)} %bitcast.7, f32[42,128]{1,0:T(8,128)} %bitcast.9, bf16[3,448,128]{2,1,0:T(8,128)(2,1)} %bitcast.8, f32[256,128]{1,0:T(8,128)} %get-tuple-element.6.cos_hbm, f32[256,128]{1,0:T(8,128)} %get-tuple-element.5.sin_hbm, f32[1,128]{1,0:T(1,128)} %bitcast.10, f32[1,128]{1,0:T(1,128)} %bitcast.11), custom_call_target="tpu_custom_call" | custom-call | tf_op jit(solution)/shard_map/layer/pallas_call | solution.py:450
  179.6 2.3 %copy.9 = bf16[1,256,2048]{2,1,0:T(8,128)(2,1)} copy(bf16[1,256,2048]{2,1,0:T(8,128)(2,1)} %bitcast.6) | data formatting | bytes 2097152
  (2 shorter events, 0.0 us)

commit v5 on v4

--- a/solution.py
+++ b/solution.py
@@ -37,7 +37,7 @@
     tok_hbm, gain_ref, shard_hbm, cos_hbm, sin_hbm, qg_ref, kg_ref,
     out_ref,
     w0, w1, w2, tok, cos_ref, sin_ref,
-    normed, spread, acc, other, q_own, q_in, kv_out, kv, relay, result,
+    normed, spread, acc, top, other, q_own, q_in, kv_out, kv, relay, result,
     local_sem, ring_send, ring_recv, tok_send, tok_recv, part_send, part_recv,
     pair_send, pair_recv, x_send, x_recv, relay_recv, out_send, out_recv,
 ):
@@ -50,18 +50,21 @@
     run = s // 2
     runs = 16
 
-    relayed = 4 * at["y"] + (at["x"] + 1) % 4
-    relay_to = (f, 2 * ((relayed + 2) % runs) + zlo)
-    relay_by = device(shifted(at, "x", -1), core)
+    def on_row(xx, yy):
+        return device({"x": (xx + 4) % 4, "y": (yy + 4) % 4, "z": at["z"]}, core)
+
+    relay_by = on_row(at["x"] - 1, at["y"] + at["x"] // 2)
+    source_x = (at["x"] + 1) % 4
+    source_y = at["y"] - source_x // 2
+    relay_from = on_row(source_x, source_y)
+    relay_to = on_row(at["x"] - 1, at["y"])
     ahead = (f, (s + 2) % (2 * runs))
     behind = (f, (s - 2 + 2 * runs) % (2 * runs))
     pair = (f, s + 1 - 2 * zlo)
-    source = (run - 2 + runs) % runs
-    relay_from = (f, 2 * (4 * (source // 4) + (source + 3) % 4) + zlo)
 
     barrier = pltpu.get_barrier_semaphore()
     peers = [device(shifted(at, d, by), core) for d in "xyz" for by in (1, -1)]
-    peers += [partner, ahead, behind, relay_to, relay_from]
+    peers += [partner, ahead, behind, relay_by, relay_from]
     for peer in peers:
         pl.semaphore_signal(barrier, inc=1, device_id=peer, device_id_type=MESH)
 
@@ -287,7 +290,7 @@
             action()
 
     has_next, has_second = run + 1 < runs, run + 2 < runs
-    relays = relayed + 2 < runs
+    relays = source_y >= 0
 
     def send_own(g):
         when(has_next, next_run(g, zlo).start)
@@ -338,43 +341,54 @@
     forward(0)
     send_own(2)
     hop(2)
+    hop(3)
     loop(4, lambda g: queries(g, True))
-
-    row = lax.broadcasted_iota(jnp.int32, (2 * rows, rows), 0) % rows
-    col = lax.broadcasted_iota(jnp.int32, (2 * rows, rows), 1)
+    loop(16, lambda h: part(h).wait_send())
+
+    row = lax.broadcasted_iota(jnp.int32, (rows, rows), 0)
+    col = lax.broadcasted_iota(jnp.int32, (rows, rows), 1)
     causal = col <= row
 
-    def two_heads(g, token_block, q, keep):
+    def score_steps(slot, g, token_block, q):
         q = q.reshape(2 * rows, 256)
         q_hi, q_lo = q[:, 0:128], q[:, 128:256]
         q = jnp.concatenate([q_hi, q_hi, q_lo, q_lo], axis=1)
         pen = [jnp.where(2 * run - 4 + token_block + m >= 0, 0.0, NEG).astype(F32)
-               for m in range(5)]
+               for m in range(4)]
+        best = []
 
         def score(m):
             keys = kv[g, token_block + m, :, 0:256]
             keys = jnp.concatenate([keys, keys], axis=1)
-            return lax.dot_general(q, keys, (((1,), (1,)), ((), ())), preferred_element_type=F32)
-
-        edge = jnp.where(causal, score(4), score(0) + pen[0])
-        inner = {m: score(m) for m in (1, 2, 3)}
-        top = jnp.max(edge, axis=-1, keepdims=True)
-        for m in inner:
-            top = jnp.maximum(top, jnp.max(inner[m], axis=-1, keepdims=True) + pen[m])
-        w_edge = jnp.exp2(edge - top)
-        w_inner = {m: jnp.exp2(inner[m] - (top - pen[m])) for m in inner}
-        total = jnp.sum(w_edge, axis=-1, keepdims=True)
-        for m in inner:
-            total = total + jnp.sum(w_inner[m], axis=-1, keepdims=True)
-        inv = 1.0 / total
-        p_edge = w_edge * inv
-        probs = [jnp.where(causal, 0.0, p_edge)] + [w_inner[m] * inv for m in inner]
-        probs.append(jnp.where(causal, p_edge, 0.0))
-        probs = jnp.concatenate([p.astype(BF16) for p in probs], axis=1)
-        values = kv[g, pl.ds(token_block, 5), :, 256:384].reshape(5 * rows, 128)
-        out = jnp.dot(probs, values, preferred_element_type=F32).astype(BF16)
-        keep[:, 0:128] = out[:rows]
-        keep[:, 128:256] = out[rows:]
+            out = lax.dot_general(q, keys, (((1,), (1,)), ((), ())), preferred_element_type=F32)
+            return out.reshape(2, rows, 256)
+
+        def tile(m):
+            if m == 0:
+                out = jnp.where(causal[None], score(4), score(0) + pen[0])
+            else:
+                out = score(m) + pen[m]
+            acc[4 * slot + m] = out
+            high = jnp.maximum(out[:, :, 0:128], out[:, :, 128:256])
+            best.append(jnp.maximum(best[-1], high) if best else high)
+            if m == 3:
+                top[slot] = jnp.broadcast_to(
+                    jnp.max(best[-1], axis=-1, keepdims=True), (2, rows, 128))
+
+        return [functools.partial(tile, m) for m in range(4)]
+
+    def value_steps(slot, g, token_block, keep):
+        def one(i):
+            high = top[slot, i, :, 0:1]
+            w = [jnp.exp2(acc[4 * slot + m, i] - high) for m in range(4)]
+            total = jnp.sum((w[0] + w[1]) + (w[2] + w[3]), axis=-1, keepdims=True)
+            probs = [jnp.where(causal, 0.0, w[0]), w[1], w[2], w[3], jnp.where(causal, w[0], 0.0)]
+            probs = jnp.concatenate([p.astype(BF16) for p in probs], axis=1)
+            values = kv[g, pl.ds(token_block, 5), :, 256:384].reshape(5 * rows, 128)
+            out = jnp.dot(probs, values, preferred_element_type=F32)
+            keep[:, 128 * i:128 * i + 128] = (out * (1.0 / total)).astype(BF16)
+
+        return [functools.partial(one, i) for i in (0, 1)]
 
     def columns(g):
         return out_ref.at[:, pl.ds(pl.multiple_of((8 * zlo + 2 * g) * 128, 256), 256)]
@@ -385,40 +399,47 @@
     def keep_own(g):
         return pltpu.make_async_copy(result.at[0, g], columns(g), local_sem.at[5 + g])
 
-    def mine_of(g):
+    def window(g):
         when(run >= 1, next_run(g, 1).wait_recv)
         when(run >= 2, second_run(g).wait_recv)
         when(run >= 2, from_relay(g).wait_recv)
-        two_heads(g, zlo, q_own[pl.ds(8 * zlo + 2 * g, 2)], result.at[0, g])
-        keep_own(g).start()
-
-    def theirs_of(g):
-        query_pair(g).wait_recv()
-        two_heads(g, 1 - zlo, q_in[pl.ds(2 * g, 2)], result.at[1, g])
-        give(g).start()
-
-    def attend(g):
-        mine_of(g)
-        theirs_of(g)
+
+    def score_mine(g):
+        return score_steps(0, g, zlo, q_own[pl.ds(8 * zlo + 2 * g, 2)])
+
+    def score_theirs(g):
+        return score_steps(1, g, 1 - zlo, q_in[pl.ds(2 * g, 2)])
+
+    def value_mine(g):
+        return value_steps(0, g, zlo, result.at[0, g])
+
+    def value_theirs(g):
+        return value_steps(1, g, 1 - zlo, result.at[1, g])
+
+    def together(scores, values):
+        for n in (0, 4, 1, 2, 5, 3):
+            steps = values if n >= 4 else scores
+            if steps:
+                steps[n % 4]()
 
     forward(1)
     send_own(3)
-    attend(0)
-    hop(3)
-    forward(2)
-    attend(1)
-    forward(3)
-    attend(2)
-    attend(3)
+    window(0)
+    together(score_mine(0), [])
+    for g in range(4):
+        query_pair(g).wait_recv()
+        together(score_theirs(g), value_mine(g))
+        keep_own(g).start()
+        if g < 2:
+            forward(g + 2)
+        if g < 3:
+            window(g + 1)
+        together(score_mine(g + 1) if g < 3 else [], value_theirs(g))
+        give(g).start()
 
     for copy in sent:
         copy.wait_send()
 
-    def drain(h, _):
-        part(h).wait_send()
-        return 0
-
-    lax.fori_loop(0, 16, drain, 0)
     for g in range(4):
         over_pair(g).wait_send()
         query_pair(g).wait_send()
@@ -461,6 +482,7 @@
             pltpu.VMEM((4, 3, rows, third), BF16),
             pltpu.VMEM((2, 2, 3, rows, third), BF16),
             pltpu.VMEM((heads, 2, rows, 256), F32),
+            pltpu.VMEM((2, 2, rows, 128), F32),
             pltpu.VMEM((heads, rows, 256), F32),
             pltpu.VMEM((heads, rows, 256), BF16),
             pltpu.VMEM((heads // 2, rows, 256), BF16),
@@ -474,7 +496,7 @@
             dma((4,)), dma((4,)),
         ],
         compiler_params=pltpu.CompilerParams(
-            collective_id=0, has_side_effects=True, vmem_limit_bytes=67043328),
+            collective_id=0, has_side_effects=True, vmem_limit_bytes=62 * 2**20),
     )(tokens[0], norm_gain.reshape(-1, 128), shard, cos, sin,
       q_gain[None], k_gain[None])
     return out[None]

time: 183 us -> 164 us (0.90)
  Pallas kernels: 176 us -> 159 us
    pallas_call x1, Pallas kernels: 176 us -> 159 us  [on_device(): pl.pallas_call(layer_kernel, name='layer', out_shape=jax.ShapeDtypeStruct...]
where the time goes in v5:
time: 164 us
  Pallas kernels  159 us (97%)
  local copies, waits for them, and re-layouts  3.21 us (2%)
  other arithmetic  2.32 us (1%)
    pallas_call x1, Pallas kernels, on_device(): pl.pallas_call(layer_kernel, name='layer', out_shape=jax.ShapeDtypeStruct...  159 us

profile of v5, /device:TPU:8, one launch (start us, length us, event | category | flops | bytes accessed | tf_op | source)
XLA Modules:
  0.0 164.3 jit_solution(4875935672970502863)
XLA Ops:
  0.0 1.3 fusion
  1.3 1.0 pad_maximum_fusion
  2.3 0.9 copy.7
  3.2 158.7 %layer.1 = bf16[256,2048]{1,0:T(8,128)(2,1)} custom-call(bf16[256,5376]{1,0:T(8,128)(2,1)} %bitcast.7, f32[42,128]{1,0:T(8,128)} %bitcast.9, bf16[3,448,128]{2,1,0:T(8,128)(2,1)} %bitcast.8, f32[256,128]{1,0:T(8,128)} %get-tuple-element.6.cos_hbm, f32[256,128]{1,0:T(8,128)} %get-tuple-element.5.sin_hbm, f32[1,128]{1,0:T(1,128)} %bitcast.10, f32[1,128]{1,0:T(1,128)} %bitcast.11), custom_call_target="tpu_custom_call" | custom-call | tf_op jit(solution)/shard_map/layer/pallas_call | solution.py:471
  162.0 2.3 %copy.9 = bf16[1,256,2048]{2,1,0:T(8,128)(2,1)} copy(bf16[1,256,2048]{2,1,0:T(8,128)(2,1)} %bitcast.6) | data formatting | bytes 2097152
  (2 shorter events, 0.0 us)

commit v6 on v5

--- a/solution.py
+++ b/solution.py
@@ -14,6 +14,8 @@
 F32 = jnp.float32
 BF16 = jnp.bfloat16
 NEG = -1e30
+LAST = 3
+STEP = 4
 
 ORDERS = (("x", "y", "z"), ("y", "z", "x"), ("z", "x", "y"))
 
@@ -94,54 +96,54 @@
 
     sent = []
 
-    def view(c, phase, index, half):
+    def block(c, phase, index, part, half):
         d1, d2, d3 = ORDERS[c]
         w = weights[c]
         if phase == 0:
             if half is None:
                 return w.at[at[d3], at[d2], index]
             return w.at[at[d3], at[d2], index, pl.ds(half * (third // 2), third // 2)]
-        if phase == 1:
-            if half is None:
-                return w.at[at[d3], index]
-            return w.at[at[d3], index, pl.ds(2 * half, 2)]
+        bundle = w.at[at[d3], index] if phase == 1 else w.at[index]
         if half is None:
-            return w.at[index]
-        return w.at[index, pl.ds(2 * half, 2)]
-
-    def ring(c, phase, step):
-        dim = ORDERS[c][phase]
-        copies = []
-        for side, by in enumerate((1, -1)):
-            if step == 0:
-                block = view(c, phase, at[dim], None)
-            else:
-                block = view(c, phase, shifted(at, dim, -by)[dim], side)
-            copies.append(pltpu.make_async_remote_copy(
-                src_ref=block, dst_ref=block,
-                send_sem=ring_send.at[c, phase, step, side],
-                recv_sem=ring_recv.at[c, phase, step, side],
-                device_id=device(shifted(at, dim, by), core), device_id_type=MESH))
-        return copies
-
-    def start(copies):
-        for copy in copies:
-            copy.start()
-        sent.extend(copies)
-
-    flying = [ring(c, 0, 0) for c in range(3)]
-    for copies in flying:
-        start(copies)
-
-    def step_ring(phase, step):
+            return bundle.at[(at[(d1, d2)[phase - 1]] + part) % 4]
+        return bundle.at[pl.ds(2 * half, 2)]
+
+    flying = {}
+
+    def send(phase, *parts):
         for c in range(3):
-            for copy in flying[c]:
-                copy.wait_recv()
-            flying[c] = ring(c, phase, step)
-            start(flying[c])
-
-    for phase, step in ((0, 1), (1, 0), (1, 1), (2, 0)):
-        step_ring(phase, step)
+            dim = ORDERS[c][phase]
+            for part in parts:
+                copies = []
+                for side, by in enumerate((1, -1)):
+                    if part == STEP:
+                        ref = block(c, phase, shifted(at, dim, -by)[dim], None, side)
+                    else:
+                        ref = block(c, phase, at[dim], part, None)
+                    copies.append(pltpu.make_async_remote_copy(
+                        src_ref=ref, dst_ref=ref,
+                        send_sem=ring_send.at[c, phase, part, side],
+                        recv_sem=ring_recv.at[c, phase, part, side],
+                        device_id=device(shifted(at, dim, by), core), device_id_type=MESH))
+                    copies[-1].start()
+                sent.extend(copies)
+                flying[c, phase, part] = copies
+
+    def receive(phase, *parts):
+        for c in range(3):
+            for part in parts:
+                for copy in flying[c, phase, part]:
+                    copy.wait_recv()
+
+    send(0, 0)
+    receive(0, 0)
+    for phase in (0, 1):
+        send(phase, STEP)
+        send(phase + 1, 0, 1, 3)
+        receive(phase, STEP)
+        send(phase + 1, 2)
+        if phase == 0:
+            receive(1, 0, 1, 3, 2)
 
     strip = 32
     for copy in fetched:
@@ -219,14 +221,13 @@
         units(yy, xx, parts, False)
         part(4 * yy + xx).start()
 
-    step_ring(2, 1)
+    receive(2, 0, 1, 3, 2)
+    send(2, STEP)
     loop(9, lambda i: units(near(y, i // 3), near(x, i % 3), [(0, zown)] + both(1) + both(2), True))
     loop(3, lambda i: units(near(y, i), far_x, [(0, zown)] + both(2), True))
     loop(3, lambda i: units(far_y, near(x, i), [(0, zown)] + both(1), True))
     units(far_y, far_x, [(0, zown)], True)
-    for copies in flying:
-        for copy in copies:
-            copy.wait_recv()
+    receive(2, STEP)
 
     def late_group(g):
         @pl.when(g != far_x)
@@ -278,11 +279,15 @@
     def second_run(g):
         return remote(kv.at[g, 2], kv.at[g, 0], x_send.at[2, g], x_recv.at[0, g], ahead)
 
-    def to_relay(g):
-        return remote(kv.at[g, 5], relay.at[g], x_send.at[3, g], relay_recv.at[g], relay_by)
-
-    def from_relay(g):
-        return remote(relay.at[g], kv.at[g, 1], x_send.at[4, g], x_recv.at[1, g], relay_to)
+    def to_relay(g, half=1):
+        slot = g + 1 - half
+        return remote(kv.at[g, 4 + half], relay.at[slot], x_send.at[3, slot],
+                      relay_recv.at[slot], relay_by)
+
+    def from_relay(g, half=1):
+        slot = g + 1 - half
+        return remote(relay.at[slot], kv.at[g, half], x_send.at[4, slot],
+                      x_recv.at[half, g], relay_to)
 
     def when(condition, action):
         @pl.when(condition)
@@ -295,15 +300,23 @@
     def send_own(g):
         when(has_next, next_run(g, zlo).start)
         when(has_second & (zlo == 1), to_relay(g).start)
+        if isinstance(g, int) and g == LAST:
+            when(has_second & (zlo == 0), to_relay(g, 0).start)
 
     def hop(g):
         over_pair(g).wait_recv()
         when(has_next, next_run(g, 1 - zlo).start)
         when(has_second & (zlo == 0), to_relay(g).start)
+        if g == LAST:
+            when(has_second & (zlo == 1), to_relay(g, 0).start)
 
     def forward(g):
-        when(run >= 1, next_run(g, 0).wait_recv)
-        when((run >= 1) & has_next, second_run(g).start)
+        if g == LAST:
+            when(relays, to_relay(g, 0).wait_recv)
+            when(relays, from_relay(g, 0).start)
+        else:
+            when(run >= 1, next_run(g, 0).wait_recv)
+            when((run >= 1) & has_next, second_run(g).start)
         when(relays, to_relay(g).wait_recv)
         when(relays, from_relay(g).start)
 
@@ -400,8 +413,10 @@
         return pltpu.make_async_copy(result.at[0, g], columns(g), local_sem.at[5 + g])
 
     def window(g):
+        if g == LAST:
+            when(run >= 1, next_run(g, 0).wait_recv)
         when(run >= 1, next_run(g, 1).wait_recv)
-        when(run >= 2, second_run(g).wait_recv)
+        when(run >= 2, from_relay(g, 0).wait_recv if g == LAST else second_run(g).wait_recv)
         when(run >= 2, from_relay(g).wait_recv)
 
     def score_mine(g):
@@ -430,8 +445,9 @@
         query_pair(g).wait_recv()
         together(score_theirs(g), value_mine(g))
         keep_own(g).start()
-        if g < 2:
-            forward(g + 2)
+        if g == 0:
+            forward(2)
+            forward(3)
         if g < 3:
             window(g + 1)
         together(score_mine(g + 1) if g < 3 else [], value_theirs(g))
@@ -445,7 +461,11 @@
         query_pair(g).wait_send()
         when(has_next, next_run(g, 0).wait_send)
         when(has_next, next_run(g, 1).wait_send)
-        when((run >= 1) & has_next, second_run(g).wait_send)
+        if g == LAST:
+            when(has_second, to_relay(g, 0).wait_send)
+            when(relays, from_relay(g, 0).wait_send)
+        else:
+            when((run >= 1) & has_next, second_run(g).wait_send)
         when(has_second, to_relay(g).wait_send)
         when(relays, from_relay(g).wait_send)
         keep_own(g).wait()
@@ -488,11 +508,11 @@
             pltpu.VMEM((heads // 2, rows, 256), BF16),
             pltpu.VMEM((4, rows, 384), BF16),
             pltpu.VMEM((4, 6, rows, 384), BF16),
-            pltpu.VMEM((4, rows, 384), BF16),
+            pltpu.VMEM((5, rows, 384), BF16),
             pltpu.VMEM((2, 4, rows, 256), BF16),
-            dma((12,)), dma((3, 3, 2, 2)), dma((3, 3, 2, 2)),
+            dma((12,)), dma((3, 3, 5, 2)), dma((3, 3, 5, 2)),
             dma((2,)), dma((2,)), dma((heads,)), dma((heads,)),
-            dma((2, 4)), dma((2, 4)), dma((5, 4)), dma((4, 4)), dma((4,)),
+            dma((2, 4)), dma((2, 4)), dma((5, 5)), dma((4, 4)), dma((5,)),
             dma((4,)), dma((4,)),
         ],
         compiler_params=pltpu.CompilerParams(

time: 164 us -> 162 us (0.988)
  Pallas kernels: 159 us -> 156 us
    pallas_call x1, Pallas kernels: 159 us -> 156 us  [on_device(): pl.pallas_call(layer_kernel, name='layer', out_shape=jax.ShapeDtypeStruct...]
where the time goes in v6:
time: 162 us
  Pallas kernels  156 us (96%)
  local copies, waits for them, and re-layouts  3.21 us (2%)
  other arithmetic  2.32 us (1%)
    pallas_call x1, Pallas kernels, on_device(): pl.pallas_call(layer_kernel, name='layer', out_shape=jax.ShapeDtypeStruct...  156 us

profile of v6, /device:TPU:8, one launch (start us, length us, event | category | flops | bytes accessed | tf_op | source)
XLA Modules:
  0.0 161.8 jit_solution(465548749905271097)
XLA Ops:
  0.0 1.3 fusion
  1.3 1.0 pad_maximum_fusion
  2.3 0.9 copy.7
  3.2 156.3 %layer.1 = bf16[256,2048]{1,0:T(8,128)(2,1)} custom-call(bf16[256,5376]{1,0:T(8,128)(2,1)} %bitcast.7, f32[42,128]{1,0:T(8,128)} %bitcast.9, bf16[3,448,128]{2,1,0:T(8,128)(2,1)} %bitcast.8, f32[256,128]{1,0:T(8,128)} %get-tuple-element.6.cos_hbm, f32[256,128]{1,0:T(8,128)} %get-tuple-element.5.sin_hbm, f32[1,128]{1,0:T(1,128)} %bitcast.10, f32[1,128]{1,0:T(1,128)} %bitcast.11), custom_call_target="tpu_custom_call" | custom-call | tf_op jit(solution)/shard_map/layer/pallas_call | solution.py:491
  159.5 2.3 %copy.9 = bf16[1,256,2048]{2,1,0:T(8,128)(2,1)} copy(bf16[1,256,2048]{2,1,0:T(8,128)(2,1)} %bitcast.6) | data formatting | bytes 2097152
  (2 shorter events, 0.0 us)

commit v7 on v6

--- a/solution.py
+++ b/solution.py
@@ -36,7 +36,7 @@
 
 
 def layer_kernel(
-    tok_hbm, gain_ref, shard_hbm, cos_hbm, sin_hbm, qg_ref, kg_ref,
+    tok_hbm, gain_ref, wq_ref, wkv_ref, cos_hbm, sin_hbm, qg_ref, kg_ref,
     out_ref,
     w0, w1, w2, tok, cos_ref, sin_ref,
     normed, spread, acc, top, other, q_own, q_in, kv_out, kv, relay, result,
@@ -85,13 +85,10 @@
     ]
     for copy in fetched:
         copy.start()
-    own = []
+    packed = jnp.concatenate([wq_ref[...], wkv_ref[...]], axis=0).astype(F32)
+    packed = jnp.concatenate([packed, jnp.zeros((128, 64), F32)], axis=1).T.astype(BF16)
     for c, (d1, d2, d3) in enumerate(ORDERS):
-        own.append(pltpu.make_async_copy(
-            shard_hbm.at[c], weights[c].at[at[d3], at[d2], at[d1]], local_sem.at[c]))
-        own[-1].start()
-    for copy in own:
-        copy.wait()
+        weights[c][at[d3], at[d2], at[d1]] = packed[c * third:(c + 1) * third]
     pl.semaphore_wait(barrier, len(peers))
 
     sent = []
@@ -395,11 +392,13 @@
             high = top[slot, i, :, 0:1]
             w = [jnp.exp2(acc[4 * slot + m, i] - high) for m in range(4)]
             total = jnp.sum((w[0] + w[1]) + (w[2] + w[3]), axis=-1, keepdims=True)
+            inv = 1.0 / total
+            w = [v * inv for v in w]
             probs = [jnp.where(causal, 0.0, w[0]), w[1], w[2], w[3], jnp.where(causal, w[0], 0.0)]
             probs = jnp.concatenate([p.astype(BF16) for p in probs], axis=1)
             values = kv[g, pl.ds(token_block, 5), :, 256:384].reshape(5 * rows, 128)
             out = jnp.dot(probs, values, preferred_element_type=F32)
-            keep[:, 128 * i:128 * i + 128] = (out * (1.0 / total)).astype(BF16)
+            keep[:, 128 * i:128 * i + 128] = out.astype(BF16)
 
         return [functools.partial(one, i) for i in (0, 1)]
 
@@ -478,7 +477,6 @@
     heads = cols * lax.axis_size("seq") // q_gain.shape[0]
     half = q_gain.shape[0] // 2
     third = quarter // 3
-    shard = jnp.concatenate([w_query, w_keyval], axis=1).reshape(3, third, 2 * cols)
     place = (lax.axis_index("seq") * rows + jnp.arange(rows)).astype(F32)
     freq = jnp.power(10000.0, -2.0 * (jnp.arange(2 * half) % half).astype(F32) / (2 * half))
     angle = place[:, None] * freq[None, :]
@@ -492,7 +490,7 @@
         layer_kernel,
         name="layer",
         out_shape=jax.ShapeDtypeStruct((rows, heads * 128), BF16),
-        in_specs=[anyspace, vmem, anyspace, anyspace, anyspace, vmem, vmem],
+        in_specs=[anyspace, vmem, vmem, vmem, anyspace, anyspace, vmem, vmem],
         out_specs=vmem,
         scratch_shapes=[
             block, block, block,
@@ -517,7 +515,7 @@
         ],
         compiler_params=pltpu.CompilerParams(
             collective_id=0, has_side_effects=True, vmem_limit_bytes=62 * 2**20),
-    )(tokens[0], norm_gain.reshape(-1, 128), shard, cos, sin,
+    )(tokens[0], norm_gain.reshape(-1, 128), w_query.T, w_keyval.T, cos, sin,
       q_gain[None], k_gain[None])
     return out[None]
 

time: 162 us -> 160 us (0.988)
  no operation moved by 1% of the time
where the time goes in v7:
time: 160 us
  Pallas kernels  156 us (98%)
  local copies, waits for them, and re-layouts  2.3 us (1%)
    pallas_call x1, Pallas kernels, on_device(): pl.pallas_call(layer_kernel, name='layer', out_shape=jax.ShapeDtypeStruct...  156 us

profile of v7, /device:TPU:8, one launch (start us, length us, event | category | flops | bytes accessed | tf_op | source)
XLA Modules:
  0.0 160.0 jit_solution(6044982731174258055)
XLA Ops:
  0.0 1.2 fusion
  1.3 156.4 %layer.1 = bf16[256,2048]{1,0:T(8,128)(2,1)} custom-call(bf16[256,5376]{1,0:T(8,128)(2,1)} %bitcast.8, f32[42,128]{1,0:T(8,128)} %bitcast.11, bf16[64,1344]{1,0:T(8,128)(2,1)} %bitcast.9, bf16[64,1344]{1,0:T(8,128)(2,1)} %bitcast.10, f32[256,128]{1,0:T(8,128)} %get-tuple-element.6.cos_hbm, f32[256,128]{1,0:T(8,128)} %get-tuple-element.5.sin_hbm, ...), custom_call_target="tpu_custom_call" | custom-call | tf_op jit(solution)/shard_map/layer/pallas_call | solution.py:489
  157.7 2.3 %copy.8 = bf16[1,256,2048]{2,1,0:T(8,128)(2,1)} copy(bf16[1,256,2048]{2,1,0:T(8,128)(2,1)} %bitcast.7) | data formatting | bytes 2097152
  (2 shorter events, 0.0 us)

commit v8 on v7

--- a/solution.py
+++ b/solution.py
@@ -439,18 +439,19 @@
     forward(1)
     send_own(3)
     window(0)
-    together(score_mine(0), [])
+    query_pair(0).wait_recv()
+    together(score_theirs(0), [])
     for g in range(4):
-        query_pair(g).wait_recv()
-        together(score_theirs(g), value_mine(g))
-        keep_own(g).start()
+        together(score_mine(g), value_theirs(g))
+        give(g).start()
         if g == 0:
             forward(2)
             forward(3)
         if g < 3:
             window(g + 1)
-        together(score_mine(g + 1) if g < 3 else [], value_theirs(g))
-        give(g).start()
+            query_pair(g + 1).wait_recv()
+        together(score_theirs(g + 1) if g < 3 else [], value_mine(g))
+        keep_own(g).start()
 
     for copy in sent:
         copy.wait_send()

time: 160 us -> 159 us (level)
  no operation moved by 1% of the time
where the time goes in v8:
time: 159 us
  Pallas kernels  155 us (97%)
  local copies, waits for them, and re-layouts  2.3 us (1%)
    pallas_call x1, Pallas kernels, on_device(): pl.pallas_call(layer_kernel, name='layer', out_shape=jax.ShapeDtypeStruct...  155 us

profile of v8, /device:TPU:8, one launch (start us, length us, event | category | flops | bytes accessed | tf_op | source)
XLA Modules:
  0.0 158.7 jit_solution(3582853266407192807)
XLA Ops:
  0.0 1.2 fusion
  1.3 155.1 %layer.1 = bf16[256,2048]{1,0:T(8,128)(2,1)} custom-call(bf16[256,5376]{1,0:T(8,128)(2,1)} %bitcast.8, f32[42,128]{1,0:T(8,128)} %bitcast.11, bf16[64,1344]{1,0:T(8,128)(2,1)} %bitcast.9, bf16[64,1344]{1,0:T(8,128)(2,1)} %bitcast.10, f32[256,128]{1,0:T(8,128)} %get-tuple-element.6.cos_hbm, f32[256,128]{1,0:T(8,128)} %get-tuple-element.5.sin_hbm, ...), custom_call_target="tpu_custom_call" | custom-call | tf_op jit(solution)/shard_map/layer/pallas_call | solution.py:490
  156.4 2.3 %copy.8 = bf16[1,256,2048]{2,1,0:T(8,128)(2,1)} copy(bf16[1,256,2048]{2,1,0:T(8,128)(2,1)} %bitcast.7) | data formatting | bytes 2097152
  (2 shorter events, 0.0 us)
